TPU v7x, 256 devices: a whole 4x4x8 slice. The times are simulated.
256 devices in a mesh: grp: 2 (over z_hi), dp: 16 (over y, z_lo), row: 8 (over x, core).
Axes of the slice: x: 4, y: 4, z: 8 (z_hi: 2, z_lo: 4; z = z_hi * 4 + z_lo), core: 2. Of those that a mesh axis runs over, the one named last changes fastest.
Arguments:
- images: bfloat16 [2, 16, 64, 256, 256], P('grp', 'dp', 'row'), may hold values from -28 to 28
- w_in: bfloat16 [2, 256, 1024], P('grp', 'dp'), may hold values from -0.375 to 0.375
- w_out: bfloat16 [2, 1024, 256], P('grp', 'dp'), may hold values from -0.1875 to 0.1875
- kernel: bfloat16 [2, 7, 7, 256], P('grp'), may hold values from -0.875 to 0.875
- gain: bfloat16 [2, 256], P('grp'), may hold values from 0.099609375 to 1.8984375
- scale: bfloat16 [2, 256], P('grp'), may hold values from 0.19921875 to 1
Outputs:
- features: bfloat16 [2, 16, 64, 256, 256], P('grp', 'dp', 'row')
- grad_w_in: float32 [2, 256, 1024], P('grp', 'dp')
- grad_w_out: float32 [2, 1024, 256], P('grp', 'dp')
- grad_kernel: float32 [2, 7, 7, 256], P('grp')
- grad_gain: float32 [2, 256], P('grp')
- grad_scale: float32 [2, 256], P('grp')
All inputs are finite; a program needn't handle non-finite values.
Results may differ from a plain program's by a relative error of at most 0.012.
Values may be sent and summed in bfloat16 or wider, within the bound.
No kernel may reach another device: no remote copies, remote signals or barrier semaphores. Data moves between devices by JAX's collectives and lax.ppermute only.
A program may use at most 128 MiB of HBM per device.

v0:
```python
import functools

import jax
import jax.numpy as jnp
from jax import lax
from jax.experimental import pallas as pl
from jax.experimental.pallas import tpu as pltpu
from jax.sharding import PartitionSpec as P


SQRT_HALF = 0.7071067811865476
INV_SQRT_TAU = 0.3989422804014327
BF = jnp.bfloat16
F32 = jnp.float32
LEFT = 8


def ring(axis, shift):
    count = lax.axis_size(axis)
    return [(i, (i + shift) % count) for i in range(count)]


def prep_kernel(images, w_in, w_out, kernel, gain, scale, head, tail, piece, small, lines, sems, *, edge):
    rows = images.shape[2]
    up = pltpu.make_async_copy(images.at[0, 0, pl.ds(0, edge)], head, sems.at[0])
    down = pltpu.make_async_copy(images.at[0, 0, pl.ds(rows - edge, edge)], tail, sems.at[1])
    up.start()
    down.start()
    me = lax.axis_index("row")
    me_x, me_c = lax.div(me, 2), lax.rem(me, 2)
    part_in = w_in[0, :, pl.ds(pl.multiple_of(128 * me, 128), 128)]
    part_out = w_out[0, pl.ds(pl.multiple_of(16 * me_x, 16), 16), pl.ds(pl.multiple_of(128 * me_c, 128), 128)]
    for q in range(piece.shape[0]):
        piece[q, :, 0:128] = part_in
        piece[q, :, 128:256] = part_out
    taps = kernel.shape[1]
    lines[...] = jnp.zeros_like(lines)
    for i in range(taps):
        lines[i * taps : i * taps + taps, :] = kernel[0, i].astype(F32)
    lines[taps * taps : taps * taps + 1, :] = gain[...].astype(F32)
    lines[taps * taps + 1 : taps * taps + 2, :] = scale[...].astype(F32)
    small[...] = lines[...].astype(BF)
    up.wait()
    down.wait()


def prep(images, w_in, w_out, kernel, gain, scale, copies):
    cols, chans = images.shape[3:]
    edge = kernel.shape[1] // 2
    anywhere = pl.BlockSpec(memory_space=pl.ANY)
    vmem = pl.BlockSpec(memory_space=pltpu.VMEM)
    return pl.pallas_call(
        functools.partial(prep_kernel, edge=edge),
        out_shape=[
            jax.ShapeDtypeStruct((edge, cols, chans), BF),
            jax.ShapeDtypeStruct((edge, cols, chans), BF),
            jax.ShapeDtypeStruct((copies, 16, 256), BF),
            jax.ShapeDtypeStruct((64, chans), BF),
        ],
        in_specs=[anywhere] + [vmem] * 5,
        out_specs=[anywhere, anywhere, vmem, vmem],
        scratch_shapes=[pltpu.VMEM((64, chans), F32), pltpu.SemaphoreType.DMA((2,))],
        name="prep",
    )(images, w_in, w_out, kernel, gain, scale)


def finish_kernel(done, grad_in, grad_out, grad_kern, grad_gain, grad_scale, lines):
    row = done.shape[0]
    taps = grad_kern.shape[1]
    for r in range(row):
        grad_in[0, :, 128 * r : 128 * r + 128] = done[r, 0:16, 0:128].astype(F32)
        x, h = r // 2, r % 2
        grad_out[0, 16 * x : 16 * x + 16, 128 * h : 128 * h + 128] = done[r, 0:16, 128:256].astype(F32)
        lines[8 * r : 8 * r + 8, :] = done[r, 16:24, :].astype(F32)
    for i in range(taps):
        grad_kern[0, i] = lines[i * taps : i * taps + taps, :]
    grad_gain[...] = lines[taps * taps : taps * taps + 1, :]
    grad_scale[...] = lines[taps * taps + 1 : taps * taps + 2, :]


def finish(done, taps):
    row, _, chans = done.shape
    return pl.pallas_call(
        finish_kernel,
        out_shape=[
            jax.ShapeDtypeStruct((1, 16, 128 * row), F32),
            jax.ShapeDtypeStruct((1, 8 * row, 256), F32),
            jax.ShapeDtypeStruct((1, taps, taps, chans), F32),
            jax.ShapeDtypeStruct((1, chans), F32),
            jax.ShapeDtypeStruct((1, chans), F32),
        ],
        scratch_shapes=[pltpu.VMEM((8 * row, chans), F32)],
        name="finish",
    )(done)


def fill_padded(pad, img, top, bot, edge):
    rows, cols, chans = img.shape
    zero = jnp.zeros((8, 128), F32)
    for cb in range(chans // 128):
        lanes = slice(cb * 128, cb * 128 + 128)
        for r in range(rows + 2 * edge):
            if r < edge:
                ref, q = top, r
            elif r < rows + edge:
                ref, q = img, r - edge
            else:
                ref, q = bot, r - rows - edge
            pad[cb, r, 0:LEFT, :] = zero
            pad[cb, r, LEFT + cols : LEFT + cols + 8, :] = zero
            pad[cb, r, LEFT : LEFT + cols, :] = ref[q, :, lanes].astype(F32)


def tree(terms):
    while len(terms) > 1:
        terms = [
            terms[a] + terms[a + 1] if a + 1 < len(terms) else terms[a] for a in range(0, len(terms), 2)
        ]
    return terms[0]


def conv_kernel(img, top, bot, own, men, filt, pad, wide_taps, *, taps):
    rows, _, _ = img.shape
    edge = taps // 2
    span = filt.shape[2]
    base = pl.program_id(0) * span

    @pl.when(pl.program_id(0) == 0)
    def _():
        fill_padded(pad, img, top, bot, edge)
        for s, small in ((0, own), (1, men)):
            lines = small[...].astype(F32)
            for q in range(taps * taps):
                wide_taps[s, q] = jnp.broadcast_to(lines[q : q + 1, :], (16, 128)).astype(BF)

    def block(wb, _):
        at = pl.multiple_of(wb * 16, 16)
        w0 = pl.multiple_of(base + at, 16)
        accs = {}
        for j in range(taps):
            vs = [
                pad[0, r, pl.ds(w0 + (LEFT - edge + j), 16), :].astype(BF) for r in range(rows + 2 * edge)
            ]
            for s in range(2):
                w = [wide_taps[s, i * taps + j] for i in range(taps)]
                for h in range(rows):
                    term = tree([vs[h + i] * w[i] for i in range(taps)]).astype(F32)
                    accs[s, h] = term if j == 0 else accs[s, h] + term
        for h in range(rows):
            for s in range(2):
                filt[s, h, pl.ds(at, 16), :] = accs[s, h]
        return 0

    lax.fori_loop(0, span // 16, block, 0)


def conv(img, top, bot, own, men, taps, cb):
    rows, cols, _ = img.shape
    edge = taps // 2
    lanes = lambda a: pl.BlockSpec(a.shape[:-1] + (128,), lambda t: (0,) * (a.ndim - 1) + (cb,))
    return pl.pallas_call(
        functools.partial(conv_kernel, taps=taps),
        out_shape=jax.ShapeDtypeStruct((2, rows, cols, 128), F32),
        grid=(4,),
        in_specs=[lanes(img), lanes(top), lanes(bot), lanes(own), lanes(men)],
        out_specs=pl.BlockSpec((2, rows, cols // 4, 128), lambda t: (0, 0, t, 0)),
        scratch_shapes=[
            pltpu.VMEM((1, rows + 2 * edge, cols + LEFT + 8, 128), F32),
            pltpu.VMEM((2, taps * taps, 16, 128), BF),
        ],
    )(img, top, bot, own, men)


def pointwise_kernel(*refs, nx, count, inv_count):
    bufs = refs[: 2 * nx]
    (filt_a, filt_b, img, own, men) = refs[2 * nx : 2 * nx + 5]
    (feat, up_conv, keep, send, gsum) = refs[2 * nx + 5 : 2 * nx + 10]
    (w_in, w_out, act, slope, g_in, g_out) = refs[2 * nx + 10 :]
    gain = own[count : count + 1, :].astype(F32)
    s_own = own[count + 1 : count + 2, :].astype(F32)
    s_men = men[count + 1 : count + 2, :].astype(F32)
    step = pl.program_id(0)
    tile, _ = img.shape
    hid = w_out.shape[2]
    dp = bufs[0].shape[0] // 2
    chunks = hid // 256
    me, me_g = lax.axis_index("row"), lax.axis_index("grp")
    me_x, me_c = lax.div(me, 2), lax.rem(me, 2)
    per_d = hid // dp

    @pl.when(step == 0)
    def _():
        for k in range(nx):
            x = lax.rem(me_x - k + nx, nx)
            for c in range(2):
                h = me_c if c == 0 else 1 - me_c
                buf = bufs[2 * k + c]
                for d in range(dp):
                    for s in range(2):
                        q = dp * (me_g if s == 0 else 1 - me_g) + d
                        w_in[s, 2 * x + h, d * 16 : d * 16 + 16, :] = buf[q, :, 0:128]
                        at = pl.multiple_of(d * per_d + x * 16, 16)
                        w_out[s, h, pl.ds(at, 16), :] = buf[q, :, 128:256]
        g_in[...] = jnp.zeros_like(g_in)
        g_out[...] = jnp.zeros_like(g_out)
        gsum[...] = jnp.zeros_like(gsum)

    def in_chunk(s, n):
        return jnp.concatenate([w_in[s, 2 * n], w_in[s, 2 * n + 1]], axis=1)

    def out_chunk(s, n):
        rows = slice(n * 256, n * 256 + 256)
        return jnp.concatenate([w_out[s, 0, rows, :], w_out[s, 1, rows, :]], axis=1)

    branch = [None, None]
    for s, small in ((0, own), (1, men)):
        x = jnp.concatenate([filt_a[s].reshape(tile, 128), filt_b[s].reshape(tile, 128)], axis=1)
        centred = x - jnp.mean(x, axis=-1, keepdims=True)
        inv = lax.rsqrt(jnp.mean(centred * centred, axis=-1, keepdims=True) + 1e-06)
        x = centred * inv
        if s == 0:
            unit, inv_std = x, inv
        x = (x * small[count : count + 1, :].astype(F32)).astype(BF)
        if s == 0:
            normed_t = x.T
        for n in range(chunks):
            pre = jnp.dot(x, in_chunk(s, n), preferred_element_type=F32)
            half_cdf = 0.5 + 0.5 * lax.erf(pre * SQRT_HALF)
            activated = (pre * half_cdf).astype(BF)
            if s == 0:
                act[:, n * 256 : n * 256 + 256] = activated
                slope[:, n * 256 : n * 256 + 256] = (
                    half_cdf + pre * jnp.exp(-0.5 * pre * pre) * INV_SQRT_TAU
                )
            part = jnp.dot(activated, out_chunk(s, n), preferred_element_type=F32)
            branch[s] = part if branch[s] is None else branch[s] + part
    scaled = branch[0] * s_own
    feat[...] = (img[...].astype(F32) + scaled).astype(BF)
    upstream = (scaled - s_men[...] * branch[1]) * inv_count
    gsum[1:2, :] = gsum[1:2, :] + jnp.sum(upstream * branch[0], axis=0, keepdims=True)
    up_branch = (upstream * s_own).astype(BF)
    up_branch_t = up_branch.T
    up_normed = None
    for n in range(chunks):
        cols = slice(n * 256, n * 256 + 256)
        g_out[:, cols] = g_out[:, cols] + jnp.dot(up_branch_t, act[:, cols], preferred_element_type=F32)
        up_active = lax.dot_general(
            up_branch, out_chunk(0, n), (((1,), (1,)), ((), ())), preferred_element_type=F32
        )
        up_pre = (up_active * slope[:, cols]).astype(BF)
        g_in[:, cols] = g_in[:, cols] + jnp.dot(normed_t, up_pre, preferred_element_type=F32)
        part = lax.dot_general(
            up_pre, in_chunk(0, n), (((1,), (1,)), ((), ())), preferred_element_type=F32
        )
        up_normed = part if up_normed is None else up_normed + part
    prod = up_normed * unit
    gsum[0:1, :] = gsum[0:1, :] + jnp.sum(prod, axis=0, keepdims=True)
    up_unit = up_normed * gain
    mean_up = jnp.mean(up_unit, axis=-1, keepdims=True)
    mean_proj = jnp.mean(prod * gain, axis=-1, keepdims=True)
    up_conv[...] = inv_std * (up_unit - mean_up - unit * mean_proj)

    @pl.when(step == pl.num_programs(0) - 1)
    def _():
        g_out_t = g_out[...].astype(BF).T
        for x in range(nx):
            for h in range(2):
                xr = lax.rem(x - me_x + nx, nx)
                lanes = slice(128 * (2 * x + h), 128 * (2 * x + h) + 128)

                def emit(out):
                    for d in range(dp):
                        out[xr, d, :, 0:128] = g_in[d * 16 : d * 16 + 16, lanes].astype(BF)
                        lo = d * per_d + 16 * x
                        out[xr, d, :, 128:256] = g_out_t[lo : lo + 16, 128 * h : 128 * h + 128]

                pl.when(me_c == h)(functools.partial(emit, keep))
                pl.when(me_c != h)(functools.partial(emit, send))


def pointwise(bufs, filt_a, filt_b, img, own, men, hid, count, inv_count):
    pixels, chans = img.shape
    _, _, cols, _ = filt_a.shape
    nx = len(bufs) // 2
    dp = bufs[0].shape[0] // 2
    tile = 512
    whole = lambda a: pl.BlockSpec(a.shape, lambda t: (0,) * a.ndim)
    lines = pl.BlockSpec((tile, chans), lambda t: (t, 0))
    filt = pl.BlockSpec((2, tile // cols, cols, 128), lambda t: (0, t, 0, 0))
    part = pl.BlockSpec((nx, dp, 16, 256), lambda t: (0, 0, 0, 0))
    return pl.pallas_call(
        functools.partial(pointwise_kernel, nx=nx, count=count, inv_count=inv_count),
        out_shape=[
            jax.ShapeDtypeStruct((pixels, chans), BF),
            jax.ShapeDtypeStruct((pixels, chans), F32),
            jax.ShapeDtypeStruct((nx, dp, 16, 256), BF),
            jax.ShapeDtypeStruct((nx, dp, 16, 256), BF),
            jax.ShapeDtypeStruct((8, chans), F32),
        ],
        grid=(pixels // tile,),
        in_specs=[whole(b) for b in bufs] + [filt, filt, lines, whole(own), whole(men)],
        out_specs=[lines, lines, part, part, pl.BlockSpec((8, chans), lambda t: (0, 0))],
        scratch_shapes=[
            pltpu.VMEM((2, hid // 128, chans, 128), BF),
            pltpu.VMEM((2, 2, hid, 128), BF),
            pltpu.VMEM((tile, hid), BF),
            pltpu.VMEM((tile, hid), F32),
            pltpu.VMEM((chans, hid), F32),
            pltpu.VMEM((chans, hid), F32),
        ],
        name="pointwise",
    )(*bufs, filt_a, filt_b, img, own, men)


def tap_grad_kernel(img, top, bot, up, gsum, out, pad, lines, *, taps):
    rows, cols, chans = img.shape
    edge = taps // 2
    fill_padded(pad, img, top, bot, edge)
    lines[...] = jnp.zeros_like(lines)
    for cb in range(chans // 128):
        lanes = slice(cb * 128, cb * 128 + 128)
        for lo, hi in ((0, 4), (4, taps)):

            def block(wb, accs):
                accs = list(accs)
                for u in range(2):
                    w0 = pl.multiple_of(wb * 32 + u * 16, 16)
                    ups = [up[h, pl.ds(w0, 16), lanes].astype(BF) for h in range(rows)]
                    for j in range(lo, hi):
                        vs = [
                            pad[cb, r, pl.ds(w0 + (LEFT - edge + j), 16), :].astype(BF)
                            for r in range(rows + 2 * edge)
                        ]
                        for i in range(taps):
                            term = tree([vs[h + i] * ups[h] for h in range(rows)]).astype(F32)
                            q = (j - lo) * taps + i
                            accs[q] = accs[q] + (term[:8] + term[8:])
                return tuple(accs)

            count = (hi - lo) * taps
            accs = lax.fori_loop(
                0, cols // 32, block, tuple(jnp.zeros((8, 128), F32) for _ in range(count))
            )
            for q in range(count):
                tap = (q % taps) * taps + lo + q // taps
                lines[tap : tap + 1, lanes] = jnp.sum(accs[q], axis=0, keepdims=True)
        for q in range(2):
            lines[taps * taps + q : taps * taps + q + 1, lanes] = gsum[q : q + 1, lanes]
    out[...] = lines[...].astype(BF)


def tap_grad(img, top, bot, up, gsum, taps):
    rows, cols, chans = img.shape
    edge = taps // 2
    return pl.pallas_call(
        functools.partial(tap_grad_kernel, taps=taps),
        out_shape=jax.ShapeDtypeStruct((64, chans), BF),
        scratch_shapes=[
            pltpu.VMEM((chans // 128, rows + 2 * edge, cols + LEFT + 8, 128), F32),
            pltpu.VMEM((64, chans), F32),
        ],
        name="tap_grad",
    )(img, top, bot, up, gsum)


def total(block):
    return jnp.sum(block.astype(F32), axis=0)


def spread(block, axis):
    copies = jnp.broadcast_to(block[None], (lax.axis_size(axis),) + block.shape)
    return lax.all_to_all(copies, axis, 0, 0, tiled=True)


def step(images, w_in, w_out, kernel, gain, scale):
    pictures = images[0, 0]
    row_count, col_count, channels = pictures.shape
    taps = kernel.shape[1]
    count = taps * taps
    dp, row, grp = lax.axis_size("dp"), lax.axis_size("row"), lax.axis_size("grp")
    nx = row // 2
    hid = w_in.shape[2]
    inv_count = 1.0 / (images.shape[1] * dp * row_count * row * col_count)
    twin = [(i, i ^ 1) for i in range(row)]
    chips = lambda k: [(i, (i + 2 * k) % row) for i in range(row)]

    head, tail, piece, small = prep(images, w_in, w_out, kernel, gain, scale, grp * dp)
    top = lax.ppermute(tail, "row", [(i, i + 1) for i in range(row - 1)])
    bot = lax.ppermute(head, "row", [(i + 1, i) for i in range(row - 1)])
    men_small = lax.ppermute(small, "grp", ring("grp", 1))
    line = lax.all_to_all(piece, ("grp", "dp"), 0, 0, tiled=True)
    hops = [line] + [lax.ppermute(line, "row", chips(k)) for k in range(1, nx)]
    bufs = []
    for block in hops:
        bufs += [block, lax.ppermute(block, "row", twin)]

    filt_a = conv(pictures, top, bot, small, men_small, taps, 0)
    filt_b = conv(pictures, top, bot, small, men_small, taps, 1)
    feat, up_conv, keep, send, gsum = pointwise(
        bufs, filt_a, filt_b, pictures.reshape(-1, channels), small, men_small, hid, count, inv_count
    )
    wide = lambda a: a.astype(F32)
    other = lax.ppermute(send, "row", twin)
    chip = (wide(keep) + wide(other)).astype(BF)
    sent = [lax.ppermute(chip[k], "row", chips(k)) for k in range(1, nx)]
    line_sum = wide(chip[0])
    for block in sent:
        line_sum = line_sum + wide(block)
    line_sum = line_sum.astype(BF)
    rest = tap_grad(pictures, top, bot, up_conv.reshape(row_count, col_count, channels), gsum, taps)
    rest = rest.reshape(row, 64 // row, channels)
    rest = total(lax.all_to_all(rest, "row", 0, 0, tiled=True)).astype(BF)
    rest = jnp.broadcast_to(rest[None], (dp,) + rest.shape)
    piece_sum = total(lax.all_to_all(jnp.concatenate([line_sum, rest], axis=1), "dp", 0, 0, tiled=True))
    grads = finish(spread(piece_sum.astype(BF), "row"), taps)
    return (feat.reshape(images.shape), *grads)


def solution(mesh):
    in_specs = (
        P("grp", "dp", "row", None, None),
        P("grp", "dp", None),
        P("grp", "dp", None),
        P("grp", None, None, None),
        P("grp", None),
        P("grp", None),
    )
    out_specs = in_specs
    return jax.shard_map(step, mesh=mesh, in_specs=in_specs, out_specs=out_specs, check_vma=False)
```

profile of v0, /device:TPU:0, one launch (start us, length us, event | category | flops | bytes accessed | tf_op | source)
XLA Modules:
  0.0 156.3 jit_solution(13900945453380579375)
XLA Ops:
  0.6 26.4 %prep.1 = (bf16[3,256,256]{2,1,0:T(8,128)(2,1)}, bf16[3,256,256]{2,1,0:T(8,128)(2,1)}, bf16[32,16,256]{2,1,0:T(8,128)(2,1)}, bf16[64,256]{1,0:T(8,128)(2,1)}) custom-call(bf16[1,1,8,256,256]{4,3,2,1,0:T(8,128)(2,1)} %images.1, bf16[1,16,1024]{2,1,0:T(8,128)(2,1)} %w_in.1, bf16[1,64,256]{2,1,0:T(8,128)(2,1)} %w_out.1, bf16[1,7,7,256]{3,2,1,0:T(8,128)(2,1)} %kernel.1, ...), custom_call_target="tpu_custom_call" | custom-call | tf_op jit(solution)/shard_map/prep/pallas_call | solution.py:52
  27.1 9.8 %all-to-all-start = ((bf16[32,16,256]{2,1,0:T(8,128)(2,1)}), bf16[32,16,256]{2,1,0:T(8,128)(2,1)S(1)}, u32[]{:S(2)}, u32[]{:S(2)}) async-start(bf16[32,16,256]{2,1,0:T(8,128)(2,1)} %get-tuple-element.20), calls=%async_computation | async-start | bytes 524288 | tf_op jit(solution)/shard_map/all_to_all | solution.py:391
  36.9 1.5 collective-permute-start.7
  38.4 12.1 %all-to-all-done.refs_0_ = bf16[32,16,256]{2,1,0:T(8,128)(2,1)S(1)} async-done(((bf16[32,16,256]{2,1,0:T(8,128)(2,1)}), bf16[32,16,256]{2,1,0:T(8,128)(2,1)S(1)}, u32[]{:S(2)}, u32[]{:S(2)}) %all-to-all-start) | async-done | bytes 262176 | tf_op jit(solution)/shard_map/all_to_all | solution.py:391
  50.5 2.8 %collective-permute-start.5 = (bf16[32,16,256]{2,1,0:T(8,128)(2,1)S(1)}, bf16[32,16,256]{2,1,0:T(8,128)(2,1)S(1)}, u32[]{:S(2)}, u32[]{:S(2)}) collective-permute-start(bf16[32,16,256]{2,1,0:T(8,128)(2,1)S(1)} %all-to-all-done.refs_0_), channel_id=1, source_target_pairs={{0,6},{1,7},{2,0},{3,1},{4,2},{5,3},{6,4},{7,5},{8,14},{9,15},{10,... | collective-permute-start | bytes 786440 | tf_op jit(solution)/shard_map/ppermute | solution.py:392
  53.2 0.8 collective-permute-start.3
  54.0 0.9 collective-permute-start.1
  54.9 0.4 collective-permute-start.9
  55.3 7.6 %collective-permute-done.9.men.refs_12_ = bf16[64,256]{1,0:T(8,128)(2,1)S(1)} collective-permute-done((bf16[64,256]{1,0:T(8,128)(2,1)}, bf16[64,256]{1,0:T(8,128)(2,1)S(1)}, u32[]{:S(2)}, u32[]{:S(2)}) %collective-permute-start.9) | collective-permute-done | bytes 32800 | tf_op jit(solution)/shard_map/ppermute | solution.py:390
  63.0 1.3 collective-permute-start.8
  64.3 0.0 collective-permute-done.7.top
  64.3 1.2 collective-permute-start
  65.5 0.0 collective-permute-done.5.refs_6_
  65.5 0.1 collective-permute-start.6
  65.6 0.0 collective-permute-done.3.refs_4_
  65.6 0.4 collective-permute-start.4
  66.0 0.2 collective-permute-done.1.refs_2_
  66.2 0.0 collective-permute-start.2
  66.2 0.6 collective-permute-done.8.bot
  66.8 0.0 copy-done.3
  66.8 0.8 copy-done.1
  67.6 6.8 %shard_map.110.refs_9_ = f32[2,8,256,128]{3,2,1,0:T(8,128)} custom-call(bf16[8,256,256]{2,1,0:T(8,128)(2,1)} %bitcast.16, bf16[3,256,256]{2,1,0:T(8,128)(2,1)} %copy-done, bf16[3,256,256]{2,1,0:T(8,128)(2,1)} %copy-done.1, bf16[64,256]{1,0:T(8,128)(2,1)} %get-tuple-element.23.own.refs_11_, bf16[64,256]{1,0:T(8,128)(2,1)} %copy-done.3), custom_call_target="tpu_custom_call" | custom-call | tf_op jit(solution)/shard_map/pallas_call | solution.py:161
  74.4 6.8 %shard_map.109.refs_8_ = f32[2,8,256,128]{3,2,1,0:T(8,128)} custom-call(bf16[8,256,256]{2,1,0:T(8,128)(2,1)} %bitcast.17, bf16[3,256,256]{2,1,0:T(8,128)(2,1)} %copy-done, bf16[3,256,256]{2,1,0:T(8,128)(2,1)} %copy-done.1, bf16[64,256]{1,0:T(8,128)(2,1)} %get-tuple-element.23.own.refs_11_, bf16[64,256]{1,0:T(8,128)(2,1)} %copy-done.3), custom_call_target="tpu_custom_call" | custom-call | tf_op jit(solution)/shard_map/pallas_call | solution.py:161
  81.2 0.0 collective-permute-done.refs_1_
  81.2 0.0 collective-permute-done.6.refs_7_
  81.3 0.0 collective-permute-done.4.refs_5_
  81.3 0.0 collective-permute-done.2.refs_3_
  81.3 0.6 copy-done.7
  81.9 0.1 copy-done.8
  82.0 0.1 copy-done.9
  82.1 0.1 copy-done.10
  82.2 19.3 %pointwise.1 = (bf16[2048,256]{1,0:T(8,128)(2,1)}, f32[2048,256]{1,0:T(8,128)}, bf16[4,16,16,256]{3,2,1,0:T(8,128)(2,1)}, bf16[4,16,16,256]{3,2,1,0:T(8,128)(2,1)}, f32[8,256]{1,0:T(8,128)}) custom-call(bf16[32,16,256]{2,1,0:T(8,128)(2,1)} %copy-done.2, bf16[32,16,256]{2,1,0:T(8,128)(2,1)} %copy-done.7, bf16[32,16,256]{2,1,0:T(8,128)(2,1)} %copy-done.6, ...), custom_call_target="tpu_custom_call" | custom-call | tf_op jit(solution)/shard_map/pointwise/pallas_call | solution.py:291
  101.6 5.9 %collective-permute-start.10 = (bf16[4,16,16,256]{3,2,1,0:T(8,128)(2,1)}, bf16[4,16,16,256]{3,2,1,0:T(8,128)(2,1)S(1)}, u32[]{:S(2)}, u32[]{:S(2)}) collective-permute-start(bf16[4,16,16,256]{3,2,1,0:T(8,128)(2,1)} %get-tuple-element.26), channel_id=1, source_target_pairs={{0,1},{1,0},{2,3},{3,2},{4,5},{5,4},{6,7},{7,6},{8,9},{9,8},{10,11... | collective-permute-start | bytes 1572872 | tf_op jit(solution)/shard_map/ppermute | solution.py:403
  107.5 1.7 %collective-permute-done.10 = bf16[4,16,16,256]{3,2,1,0:T(8,128)(2,1)S(1)} collective-permute-done((bf16[4,16,16,256]{3,2,1,0:T(8,128)(2,1)}, bf16[4,16,16,256]{3,2,1,0:T(8,128)(2,1)S(1)}, u32[]{:S(2)}, u32[]{:S(2)}) %collective-permute-start.10) | collective-permute-done | bytes 524320 | tf_op jit(solution)/shard_map/ppermute | solution.py:403
  109.2 1.2 add_convert_fusion
  110.5 0.3 collective-permute-start.11
  110.7 3.0 %collective-permute-start.13 = (bf16[16,16,256]{2,1,0:T(8,128)(2,1)S(1)}, bf16[16,16,256]{2,1,0:T(8,128)(2,1)S(1)}, u32[]{:S(2)}, u32[]{:S(2)}) collective-permute-start(bf16[16,16,256]{2,1,0:T(8,128)(2,1)S(1)} %get-tuple-element.41), channel_id=1, source_target_pairs={{0,6},{1,7},{2,0},{3,1},{4,2},{5,3},{6,4},{7,5},{8,14},{9,15},{10,... | collective-permute-start | bytes 393224 | tf_op jit(solution)/shard_map/ppermute | solution.py:405
  113.8 0.8 collective-permute-start.12
  114.6 7.8 %tap_grad.1 = bf16[64,256]{1,0:T(8,128)(2,1)} custom-call(bf16[8,256,256]{2,1,0:T(8,128)(2,1)} %bitcast.19, bf16[3,256,256]{2,1,0:T(8,128)(2,1)} %copy-done, bf16[3,256,256]{2,1,0:T(8,128)(2,1)} %copy-done.1, f32[8,256,256]{2,1,0:T(8,128)} %bitcast.20, f32[8,256]{1,0:T(8,128)} %get-tuple-element.28.gsum), custom_call_target="tpu_custom_call" | custom-call | tf_op jit(solution)/shard_map/tap_grad/pallas_call | solution.py:355
  122.4 9.4 %all_to_all.20 = bf16[8,8,256]{2,1,0:T(8,128)(2,1)S(1)} all-to-all(bf16[8,8,256]{2,1,0:T(8,128)(2,1)} %bitcast.21), channel_id=1, replica_groups=mesh['grp'=2,'dp'=16,'row'=8] {'row'}, dimensions={0} | all-to-all | bytes 65536 | tf_op jit(solution)/shard_map/all_to_all | solution.py:412
  131.9 0.0 collective-permute-done.11
  131.9 0.0 collective-permute-done.13
  131.9 0.0 collective-permute-done.12
  131.9 0.1 fusion.2
  132.0 12.3 %all_to_all.21 = bf16[16,24,256]{2,1,0:T(8,128)(2,1)S(1)} all-to-all(bf16[16,24,256]{2,1,0:T(8,128)(2,1)S(1)} %pad_maximum_fusion), channel_id=1, replica_groups=mesh['grp'=2,'dp'=16,'row'=8] {'dp'}, dimensions={0} | all-to-all | bytes 393216 | tf_op jit(solution)/shard_map/all_to_all | solution.py:414
  144.4 8.9 %all_to_all.22.done = bf16[8,24,256]{2,1,0:T(8,128)(2,1)} all-to-all(bf16[8,24,256]{2,1,0:T(8,128)(2,1)S(1)} %broadcast_in_dim.5), channel_id=1, replica_groups=mesh['grp'=2,'dp'=16,'row'=8] {'row'}, dimensions={0} | all-to-all | bytes 196608 | tf_op jit(solution)/shard_map/all_to_all | solution.py:372
  153.2 1.6 %finish.1 = (f32[1,16,1024]{2,1,0:T(8,128)}, f32[1,64,256]{2,1,0:T(8,128)}, f32[1,7,7,256]{3,2,1,0:T(8,128)}, f32[1,256]{1,0:T(1,128)}, f32[1,256]{1,0:T(1,128)}) custom-call(bf16[8,24,256]{2,1,0:T(8,128)(2,1)} %all_to_all.22.done), custom_call_target="tpu_custom_call" | custom-call | tf_op jit(solution)/shard_map/finish/pallas_call | solution.py:83
  154.8 1.5 copy.12
  (22 shorter events, 0.1 us)
Async XLA Ops:
  27.1 23.4 %all-to-all-start = ((bf16[32,16,256]{2,1,0:T(8,128)(2,1)}), bf16[32,16,256]{2,1,0:T(8,128)(2,1)S(1)}, u32[]{:S(2)}, u32[]{:S(2)}) async-start(bf16[32,16,256]{2,1,0:T(8,128)(2,1)} %get-tuple-element.20), calls=%async_computation | async-start | bytes 524288 | tf_op jit(solution)/shard_map/all_to_all | solution.py:391
  36.9 27.4 %collective-permute-start.7 = (bf16[3,256,256]{2,1,0:T(8,128)(2,1)}, bf16[3,256,256]{2,1,0:T(8,128)(2,1)S(1)}, u32[]{:S(2)}, u32[]{:S(2)}) collective-permute-start(bf16[3,256,256]{2,1,0:T(8,128)(2,1)} %get-tuple-element.21), channel_id=1, source_target_pairs={{0,1},{1,2},{2,3},{3,4},{4,5},{5,6},{6,7},{8,9},{9,10},{10,11},{11... | collective-permute-start | bytes 1179656 | tf_op jit(solution)/shard_map/ppermute | solution.py:388
  50.5 30.8 %copy-start.2 = (bf16[32,16,256]{2,1,0:T(8,128)(2,1)}, bf16[32,16,256]{2,1,0:T(8,128)(2,1)S(1)}, u32[]{:S(2)}) copy-start(bf16[32,16,256]{2,1,0:T(8,128)(2,1)S(1)} %all-to-all-done.refs_0_) | copy-start | bytes 786436
  50.5 15.0 %collective-permute-start.5 = (bf16[32,16,256]{2,1,0:T(8,128)(2,1)S(1)}, bf16[32,16,256]{2,1,0:T(8,128)(2,1)S(1)}, u32[]{:S(2)}, u32[]{:S(2)}) collective-permute-start(bf16[32,16,256]{2,1,0:T(8,128)(2,1)S(1)} %all-to-all-done.refs_0_), channel_id=1, source_target_pairs={{0,6},{1,7},{2,0},{3,1},{4,2},{5,3},{6,4},{7,5},{8,14},{9,15},{10,... | collective-permute-start | bytes 786440 | tf_op jit(solution)/shard_map/ppermute | solution.py:392
  53.2 12.4 %collective-permute-start.3 = (bf16[32,16,256]{2,1,0:T(8,128)(2,1)S(1)}, bf16[32,16,256]{2,1,0:T(8,128)(2,1)S(1)}, u32[]{:S(2)}, u32[]{:S(2)}) collective-permute-start(bf16[32,16,256]{2,1,0:T(8,128)(2,1)S(1)} %all-to-all-done.refs_0_), channel_id=1, source_target_pairs={{0,4},{1,5},{2,6},{3,7},{4,0},{5,1},{6,2},{7,3},{8,12},{9,13},{10,... | collective-permute-start | bytes 786440 | tf_op jit(solution)/shard_map/ppermute | solution.py:392
  54.0 12.2 %collective-permute-start.1 = (bf16[32,16,256]{2,1,0:T(8,128)(2,1)S(1)}, bf16[32,16,256]{2,1,0:T(8,128)(2,1)S(1)}, u32[]{:S(2)}, u32[]{:S(2)}) collective-permute-start(bf16[32,16,256]{2,1,0:T(8,128)(2,1)S(1)} %all-to-all-done.refs_0_), channel_id=1, source_target_pairs={{0,2},{1,3},{2,4},{3,5},{4,6},{5,7},{6,0},{7,1},{8,10},{9,11},{10,... | collective-permute-start | bytes 786440 | tf_op jit(solution)/shard_map/ppermute | solution.py:392
  54.9 8.0 %collective-permute-start.9 = (bf16[64,256]{1,0:T(8,128)(2,1)}, bf16[64,256]{1,0:T(8,128)(2,1)S(1)}, u32[]{:S(2)}, u32[]{:S(2)}) collective-permute-start(bf16[64,256]{1,0:T(8,128)(2,1)} %get-tuple-element.23.own.refs_11_), channel_id=1, source_target_pairs={{0,128},{128,0},{1,129},{129,1},{2,130},{130,2},{3,131},{131,3},{4... | collective-permute-start | bytes 98312 | tf_op jit(solution)/shard_map/ppermute | solution.py:390
  63.0 3.8 %copy-start.3 = (bf16[64,256]{1,0:T(8,128)(2,1)}, bf16[64,256]{1,0:T(8,128)(2,1)S(1)}, u32[]{:S(2)}) copy-start(bf16[64,256]{1,0:T(8,128)(2,1)S(1)} %collective-permute-done.9.men.refs_12_) | copy-start | bytes 98308
  63.0 3.8 %collective-permute-start.8 = (bf16[3,256,256]{2,1,0:T(8,128)(2,1)}, bf16[3,256,256]{2,1,0:T(8,128)(2,1)S(1)}, u32[]{:S(2)}, u32[]{:S(2)}) collective-permute-start(bf16[3,256,256]{2,1,0:T(8,128)(2,1)} %get-tuple-element.22), channel_id=1, source_target_pairs={{1,0},{2,1},{3,2},{4,3},{5,4},{6,5},{7,6},{9,8},{10,9},{11,10},{12... | collective-permute-start | bytes 1179656 | tf_op jit(solution)/shard_map/ppermute | solution.py:389
  64.3 2.5 %copy-start = (bf16[3,256,256]{2,1,0:T(8,128)(2,1)}, bf16[3,256,256]{2,1,0:T(8,128)(2,1)S(1)}, u32[]{:S(2)}) copy-start(bf16[3,256,256]{2,1,0:T(8,128)(2,1)S(1)} %collective-permute-done.7.top) | copy-start | bytes 1179652
  64.3 17.0 %collective-permute-start = (bf16[32,16,256]{2,1,0:T(8,128)(2,1)S(1)}, bf16[32,16,256]{2,1,0:T(8,128)(2,1)S(1)}, u32[]{:S(2)}, u32[]{:S(2)}) collective-permute-start(bf16[32,16,256]{2,1,0:T(8,128)(2,1)S(1)} %all-to-all-done.refs_0_), channel_id=1, source_target_pairs={{0,1},{1,0},{2,3},{3,2},{4,5},{5,4},{6,7},{7,6},{8,9},{9,8},{10,11... | collective-permute-start | bytes 786440 | tf_op jit(solution)/shard_map/ppermute | solution.py:395
  65.5 15.8 %copy-start.4 = (bf16[32,16,256]{2,1,0:T(8,128)(2,1)}, bf16[32,16,256]{2,1,0:T(8,128)(2,1)S(1)}, u32[]{:S(2)}) copy-start(bf16[32,16,256]{2,1,0:T(8,128)(2,1)S(1)} %collective-permute-done.5.refs_6_) | copy-start | bytes 786436
  65.5 15.8 %collective-permute-start.6 = (bf16[32,16,256]{2,1,0:T(8,128)(2,1)S(1)}, bf16[32,16,256]{2,1,0:T(8,128)(2,1)S(1)}, u32[]{:S(2)}, u32[]{:S(2)}) collective-permute-start(bf16[32,16,256]{2,1,0:T(8,128)(2,1)S(1)} %collective-permute-done.5.refs_6_), channel_id=1, source_target_pairs={{0,1},{1,0},{2,3},{3,2},{4,5},{5,4},{6,7},{7,6},{8,9},{9,8},{10,11... | collective-permute-start | bytes 786440 | tf_op jit(solution)/shard_map/ppermute | solution.py:395
  65.6 15.7 %copy-start.5 = (bf16[32,16,256]{2,1,0:T(8,128)(2,1)}, bf16[32,16,256]{2,1,0:T(8,128)(2,1)S(1)}, u32[]{:S(2)}) copy-start(bf16[32,16,256]{2,1,0:T(8,128)(2,1)S(1)} %collective-permute-done.3.refs_4_) | copy-start | bytes 786436
  65.6 15.7 %collective-permute-start.4 = (bf16[32,16,256]{2,1,0:T(8,128)(2,1)S(1)}, bf16[32,16,256]{2,1,0:T(8,128)(2,1)S(1)}, u32[]{:S(2)}, u32[]{:S(2)}) collective-permute-start(bf16[32,16,256]{2,1,0:T(8,128)(2,1)S(1)} %collective-permute-done.3.refs_4_), channel_id=1, source_target_pairs={{0,1},{1,0},{2,3},{3,2},{4,5},{5,4},{6,7},{7,6},{8,9},{9,8},{10,11... | collective-permute-start | bytes 786440 | tf_op jit(solution)/shard_map/ppermute | solution.py:395
  66.2 15.1 %copy-start.6 = (bf16[32,16,256]{2,1,0:T(8,128)(2,1)}, bf16[32,16,256]{2,1,0:T(8,128)(2,1)S(1)}, u32[]{:S(2)}) copy-start(bf16[32,16,256]{2,1,0:T(8,128)(2,1)S(1)} %collective-permute-done.1.refs_2_) | copy-start | bytes 786436
  66.2 15.1 %collective-permute-start.2 = (bf16[32,16,256]{2,1,0:T(8,128)(2,1)S(1)}, bf16[32,16,256]{2,1,0:T(8,128)(2,1)S(1)}, u32[]{:S(2)}, u32[]{:S(2)}) collective-permute-start(bf16[32,16,256]{2,1,0:T(8,128)(2,1)S(1)} %collective-permute-done.1.refs_2_), channel_id=1, source_target_pairs={{0,1},{1,0},{2,3},{3,2},{4,5},{5,4},{6,7},{7,6},{8,9},{9,8},{10,11... | collective-permute-start | bytes 786440 | tf_op jit(solution)/shard_map/ppermute | solution.py:395
  66.8 0.8 copy-start.1
  81.2 0.7 copy-start.7
  81.3 0.8 copy-start.8
  81.3 0.8 copy-start.9
  81.3 0.9 copy-start.10
  101.6 7.7 %collective-permute-start.10 = (bf16[4,16,16,256]{3,2,1,0:T(8,128)(2,1)}, bf16[4,16,16,256]{3,2,1,0:T(8,128)(2,1)S(1)}, u32[]{:S(2)}, u32[]{:S(2)}) collective-permute-start(bf16[4,16,16,256]{3,2,1,0:T(8,128)(2,1)} %get-tuple-element.26), channel_id=1, source_target_pairs={{0,1},{1,0},{2,3},{3,2},{4,5},{5,4},{6,7},{7,6},{8,9},{9,8},{10,11... | collective-permute-start | bytes 1572872 | tf_op jit(solution)/shard_map/ppermute | solution.py:403
  110.5 21.4 %collective-permute-start.11 = (bf16[16,16,256]{2,1,0:T(8,128)(2,1)S(1)}, bf16[16,16,256]{2,1,0:T(8,128)(2,1)S(1)}, u32[]{:S(2)}, u32[]{:S(2)}) collective-permute-start(bf16[16,16,256]{2,1,0:T(8,128)(2,1)S(1)} %get-tuple-element.40), channel_id=1, source_target_pairs={{0,2},{1,3},{2,4},{3,5},{4,6},{5,7},{6,0},{7,1},{8,10},{9,11},{10,... | collective-permute-start | bytes 393224 | tf_op jit(solution)/shard_map/ppermute | solution.py:405
  110.7 21.2 %collective-permute-start.13 = (bf16[16,16,256]{2,1,0:T(8,128)(2,1)S(1)}, bf16[16,16,256]{2,1,0:T(8,128)(2,1)S(1)}, u32[]{:S(2)}, u32[]{:S(2)}) collective-permute-start(bf16[16,16,256]{2,1,0:T(8,128)(2,1)S(1)} %get-tuple-element.41), channel_id=1, source_target_pairs={{0,6},{1,7},{2,0},{3,1},{4,2},{5,3},{6,4},{7,5},{8,14},{9,15},{10,... | collective-permute-start | bytes 393224 | tf_op jit(solution)/shard_map/ppermute | solution.py:405
  113.8 18.1 %collective-permute-start.12 = (bf16[16,16,256]{2,1,0:T(8,128)(2,1)S(1)}, bf16[16,16,256]{2,1,0:T(8,128)(2,1)S(1)}, u32[]{:S(2)}, u32[]{:S(2)}) collective-permute-start(bf16[16,16,256]{2,1,0:T(8,128)(2,1)S(1)} %get-tuple-element.42), channel_id=1, source_target_pairs={{0,4},{1,5},{2,6},{3,7},{4,0},{5,1},{6,2},{7,3},{8,12},{9,13},{10,... | collective-permute-start | bytes 393224 | tf_op jit(solution)/shard_map/ppermute | solution.py:405
where the time goes:
time: 159 us; the launch traced here: 156 us
  Pallas kernels  68.9 us (43%)
  blocking collectives  30.6 us (19%)
  starting transfers between devices  29.2 us (18%)
  waiting for transfers between devices  22.3 us (14%)
  local copies, waits for them, and re-layouts  3.21 us (2%)
    pallas_call x1, Pallas kernels, prep(): pl.pallas_call(functools.partial(prep_kernel, edge=edge), out_shape=[jax....  26.4 us
    pallas_call x1, Pallas kernels, pointwise(): pl.pallas_call(functools.partial(pointwise_kernel, nx=nx, count=count, in...  19.3 us
    pallas_call x2, Pallas kernels, conv(): pl.pallas_call(functools.partial(conv_kernel, taps=taps), out_shape=jax.S...  13.7 us
    all_to_all x1, blocking collectives, step(): lax.all_to_all(jnp.concatenate([line_sum, rest], axis=1), 'dp', 0, 0, til...  12.3 us
    all_to_all x1, waiting for transfers between devices, step(): line = lax.all_to_all(piece, ('grp', 'dp'), 0, 0, tiled=True)  12.1 us
    all_to_all x1, starting transfers between devices, step(): line = lax.all_to_all(piece, ('grp', 'dp'), 0, 0, tiled=True)  9.79 us
    all_to_all x1, blocking collectives, step(): rest = total(lax.all_to_all(rest, 'row', 0, 0, tiled=True)).astype(BF)  9.45 us
    all_to_all x1, blocking collectives, spread(): return lax.all_to_all(copies, axis, 0, 0, tiled=True)  8.86 us
  transfers between devices with their start and end apart: 15, of which 5 were waited for; matrix products, arithmetic and copies ran while one was open for 0% of the time, Pallas kernels for 14%

commit v1 on v0

--- a/solution.py
+++ b/solution.py
@@ -58,7 +58,7 @@
             jax.ShapeDtypeStruct((64, chans), BF),
         ],
         in_specs=[anywhere] + [vmem] * 5,
-        out_specs=[anywhere, anywhere, vmem, vmem],
+        out_specs=[vmem] * 4,
         scratch_shapes=[pltpu.VMEM((64, chans), F32), pltpu.SemaphoreType.DMA((2,))],
         name="prep",
     )(images, w_in, w_out, kernel, gain, scale)
@@ -66,14 +66,14 @@
 
 def finish_kernel(done, grad_in, grad_out, grad_kern, grad_gain, grad_scale, lines):
     row = done.shape[0]
-    taps = grad_kern.shape[1]
+    taps = grad_kern.shape[0]
     for r in range(row):
         grad_in[0, :, 128 * r : 128 * r + 128] = done[r, 0:16, 0:128].astype(F32)
         x, h = r // 2, r % 2
         grad_out[0, 16 * x : 16 * x + 16, 128 * h : 128 * h + 128] = done[r, 0:16, 128:256].astype(F32)
         lines[8 * r : 8 * r + 8, :] = done[r, 16:24, :].astype(F32)
-    for i in range(taps):
-        grad_kern[0, i] = lines[i * taps : i * taps + taps, :]
+    for q in range(taps * taps):
+        grad_kern[q // taps, q % taps] = lines[q : q + 1, :]
     grad_gain[...] = lines[taps * taps : taps * taps + 1, :]
     grad_scale[...] = lines[taps * taps + 1 : taps * taps + 2, :]
 
@@ -85,7 +85,7 @@
         out_shape=[
             jax.ShapeDtypeStruct((1, 16, 128 * row), F32),
             jax.ShapeDtypeStruct((1, 8 * row, 256), F32),
-            jax.ShapeDtypeStruct((1, taps, taps, chans), F32),
+            jax.ShapeDtypeStruct((taps, taps, 1, chans), F32),
             jax.ShapeDtypeStruct((1, chans), F32),
             jax.ShapeDtypeStruct((1, chans), F32),
         ],
@@ -412,8 +412,8 @@
     rest = total(lax.all_to_all(rest, "row", 0, 0, tiled=True)).astype(BF)
     rest = jnp.broadcast_to(rest[None], (dp,) + rest.shape)
     piece_sum = total(lax.all_to_all(jnp.concatenate([line_sum, rest], axis=1), "dp", 0, 0, tiled=True))
-    grads = finish(spread(piece_sum.astype(BF), "row"), taps)
-    return (feat.reshape(images.shape), *grads)
+    grad_in, grad_out, grad_kern, *rest = finish(spread(piece_sum.astype(BF), "row"), taps)
+    return (feat.reshape(images.shape), grad_in, grad_out, grad_kern.transpose(2, 0, 1, 3), *rest)
 
 
 def solution(mesh):

time: 159 us -> 134 us (0.84)
  the two profiles are of different devices: /device:TPU:0 before, /device:TPU:1 now
where the time goes in v1:
time: 134 us
  Pallas kernels  45.3 us (34%)
  starting transfers between devices  32.4 us (24%)
  blocking collectives  30.8 us (23%)
  waiting for transfers between devices  21.3 us (16%)
  local copies, waits for them, and re-layouts  1.72 us (1%)
    pallas_call x1, Pallas kernels, pointwise(): pl.pallas_call(functools.partial(pointwise_kernel, nx=nx, count=count, in...  19.3 us
    pallas_call x2, Pallas kernels, conv(): pl.pallas_call(functools.partial(conv_kernel, taps=taps), out_shape=jax.S...  13.7 us
    all_to_all x1, starting transfers between devices, step(): line = lax.all_to_all(piece, ('grp', 'dp'), 0, 0, tiled=True)  12 us
    all_to_all x1, blocking collectives, spread(): return lax.all_to_all(copies, axis, 0, 0, tiled=True)  11 us
    all_to_all x1, blocking collectives, step(): lax.all_to_all(jnp.concatenate([line_sum, rest], axis=1), 'dp', 0, 0, til...  10.1 us
    all_to_all x1, blocking collectives, step(): rest = total(lax.all_to_all(rest, 'row', 0, 0, tiled=True)).astype(BF)  9.69 us
    all_to_all x1, waiting for transfers between devices, step(): line = lax.all_to_all(piece, ('grp', 'dp'), 0, 0, tiled=True)  8 us
    pallas_call x1, Pallas kernels, tap_grad(): pl.pallas_call(functools.partial(tap_grad_kernel, taps=taps), out_shape=j...  7.85 us
  transfers between devices with their start and end apart: 15, of which 4 were waited for; matrix products, arithmetic and copies ran while one was open for 0% of the time, Pallas kernels for 16%

profile of v1, /device:TPU:1, one launch (start us, length us, event | category | flops | bytes accessed | tf_op | source)
XLA Modules:
  0.0 133.6 jit_solution(12323811465379808076)
XLA Ops:
  0.6 2.9 %prep.1 = (bf16[3,256,256]{2,1,0:T(8,128)(2,1)}, bf16[3,256,256]{2,1,0:T(8,128)(2,1)}, bf16[32,16,256]{2,1,0:T(8,128)(2,1)}, bf16[64,256]{1,0:T(8,128)(2,1)}) custom-call(bf16[1,1,8,256,256]{4,3,2,1,0:T(8,128)(2,1)} %images.1, bf16[1,16,1024]{2,1,0:T(8,128)(2,1)} %w_in.1, bf16[1,64,256]{2,1,0:T(8,128)(2,1)} %w_out.1, bf16[1,7,7,256]{3,2,1,0:T(8,128)(2,1)} %kernel.1, ...), custom_call_target="tpu_custom_call" | custom-call | tf_op jit(solution)/shard_map/prep/pallas_call | solution.py:52
  3.5 12.0 %all-to-all-start = ((bf16[32,16,256]{2,1,0:T(8,128)(2,1)}), bf16[32,16,256]{2,1,0:T(8,128)(2,1)S(1)}, u32[]{:S(2)}, u32[]{:S(2)}) async-start(bf16[32,16,256]{2,1,0:T(8,128)(2,1)} %get-tuple-element.20), calls=%async_computation | async-start | bytes 524288 | tf_op jit(solution)/shard_map/all_to_all | solution.py:391
  15.6 4.0 %collective-permute-start.7 = (bf16[3,256,256]{2,1,0:T(8,128)(2,1)}, bf16[3,256,256]{2,1,0:T(8,128)(2,1)S(1)}, u32[]{:S(2)}, u32[]{:S(2)}) collective-permute-start(bf16[3,256,256]{2,1,0:T(8,128)(2,1)} %get-tuple-element.21), channel_id=1, source_target_pairs={{0,1},{1,2},{2,3},{3,4},{4,5},{5,6},{6,7},{8,9},{9,10},{10,11},{11... | collective-permute-start | bytes 1179656 | tf_op jit(solution)/shard_map/ppermute | solution.py:388
  19.5 8.0 %all-to-all-done.refs_0_ = bf16[32,16,256]{2,1,0:T(8,128)(2,1)S(1)} async-done(((bf16[32,16,256]{2,1,0:T(8,128)(2,1)}), bf16[32,16,256]{2,1,0:T(8,128)(2,1)S(1)}, u32[]{:S(2)}, u32[]{:S(2)}) %all-to-all-start) | async-done | bytes 262176 | tf_op jit(solution)/shard_map/all_to_all | solution.py:391
  27.5 2.5 %collective-permute-start.5 = (bf16[32,16,256]{2,1,0:T(8,128)(2,1)S(1)}, bf16[32,16,256]{2,1,0:T(8,128)(2,1)S(1)}, u32[]{:S(2)}, u32[]{:S(2)}) collective-permute-start(bf16[32,16,256]{2,1,0:T(8,128)(2,1)S(1)} %all-to-all-done.refs_0_), channel_id=1, source_target_pairs={{0,6},{1,7},{2,0},{3,1},{4,2},{5,3},{6,4},{7,5},{8,14},{9,15},{10,... | collective-permute-start | bytes 786440 | tf_op jit(solution)/shard_map/ppermute | solution.py:392
  30.0 0.5 collective-permute-start.3
  30.5 0.6 collective-permute-start.1
  31.1 1.5 %collective-permute-start.9 = (bf16[64,256]{1,0:T(8,128)(2,1)}, bf16[64,256]{1,0:T(8,128)(2,1)S(1)}, u32[]{:S(2)}, u32[]{:S(2)}) collective-permute-start(bf16[64,256]{1,0:T(8,128)(2,1)} %get-tuple-element.23.own.refs_11_), channel_id=1, source_target_pairs={{0,128},{128,0},{1,129},{129,1},{2,130},{130,2},{3,131},{131,3},{4... | collective-permute-start | bytes 98312 | tf_op jit(solution)/shard_map/ppermute | solution.py:390
  32.6 5.4 %collective-permute-done.9.men.refs_12_ = bf16[64,256]{1,0:T(8,128)(2,1)S(1)} collective-permute-done((bf16[64,256]{1,0:T(8,128)(2,1)}, bf16[64,256]{1,0:T(8,128)(2,1)S(1)}, u32[]{:S(2)}, u32[]{:S(2)}) %collective-permute-start.9) | collective-permute-done | bytes 32800 | tf_op jit(solution)/shard_map/ppermute | solution.py:390
  38.0 6.5 %collective-permute-start.8 = (bf16[3,256,256]{2,1,0:T(8,128)(2,1)}, bf16[3,256,256]{2,1,0:T(8,128)(2,1)S(1)}, u32[]{:S(2)}, u32[]{:S(2)}) collective-permute-start(bf16[3,256,256]{2,1,0:T(8,128)(2,1)} %get-tuple-element.22), channel_id=1, source_target_pairs={{1,0},{2,1},{3,2},{4,3},{5,4},{6,5},{7,6},{9,8},{10,9},{11,10},{12... | collective-permute-start | bytes 1179656 | tf_op jit(solution)/shard_map/ppermute | solution.py:389
  44.5 0.0 collective-permute-done.7.top
  44.5 0.1 collective-permute-start
  44.6 0.0 collective-permute-done.5.refs_6_
  44.7 0.5 collective-permute-start.6
  45.1 0.0 collective-permute-done.3.refs_4_
  45.1 0.1 collective-permute-start.4
  45.3 0.0 collective-permute-done.1.refs_2_
  45.3 0.6 collective-permute-start.2
  45.9 5.7 %collective-permute-done.8.bot = bf16[3,256,256]{2,1,0:T(8,128)(2,1)S(1)} collective-permute-done((bf16[3,256,256]{2,1,0:T(8,128)(2,1)}, bf16[3,256,256]{2,1,0:T(8,128)(2,1)S(1)}, u32[]{:S(2)}, u32[]{:S(2)}) %collective-permute-start.8) | collective-permute-done | bytes 393248 | tf_op jit(solution)/shard_map/ppermute | solution.py:389
  51.6 0.0 copy-done
  51.6 0.8 copy-done.1
  52.4 6.8 %shard_map.110.refs_9_ = f32[2,8,256,128]{3,2,1,0:T(8,128)} custom-call(bf16[8,256,256]{2,1,0:T(8,128)(2,1)} %bitcast.17, bf16[3,256,256]{2,1,0:T(8,128)(2,1)} %copy-done, bf16[3,256,256]{2,1,0:T(8,128)(2,1)} %copy-done.1, bf16[64,256]{1,0:T(8,128)(2,1)} %get-tuple-element.23.own.refs_11_, bf16[64,256]{1,0:T(8,128)(2,1)} %copy-done.3), custom_call_target="tpu_custom_call" | custom-call | tf_op jit(solution)/shard_map/pallas_call | solution.py:161
  59.2 6.8 %shard_map.109.refs_8_ = f32[2,8,256,128]{3,2,1,0:T(8,128)} custom-call(bf16[8,256,256]{2,1,0:T(8,128)(2,1)} %bitcast.18, bf16[3,256,256]{2,1,0:T(8,128)(2,1)} %copy-done, bf16[3,256,256]{2,1,0:T(8,128)(2,1)} %copy-done.1, bf16[64,256]{1,0:T(8,128)(2,1)} %get-tuple-element.23.own.refs_11_, bf16[64,256]{1,0:T(8,128)(2,1)} %copy-done.3), custom_call_target="tpu_custom_call" | custom-call | tf_op jit(solution)/shard_map/pallas_call | solution.py:161
  66.0 0.0 collective-permute-done.refs_1_
  66.0 0.0 collective-permute-done.6.refs_7_
  66.1 0.0 collective-permute-done.4.refs_5_
  66.1 0.0 collective-permute-done.2.refs_3_
  66.1 0.0 copy-start.10
  66.1 0.6 copy-done.7
  66.7 0.1 copy-done.8
  66.8 0.1 copy-done.9
  66.9 0.1 copy-done.10
  67.0 19.3 %pointwise.1 = (bf16[2048,256]{1,0:T(8,128)(2,1)}, f32[2048,256]{1,0:T(8,128)}, bf16[4,16,16,256]{3,2,1,0:T(8,128)(2,1)}, bf16[4,16,16,256]{3,2,1,0:T(8,128)(2,1)}, f32[8,256]{1,0:T(8,128)}) custom-call(bf16[32,16,256]{2,1,0:T(8,128)(2,1)} %copy-done.2, bf16[32,16,256]{2,1,0:T(8,128)(2,1)} %copy-done.7, bf16[32,16,256]{2,1,0:T(8,128)(2,1)} %copy-done.6, ...), custom_call_target="tpu_custom_call" | custom-call | tf_op jit(solution)/shard_map/pointwise/pallas_call | solution.py:291
  86.4 0.3 collective-permute-start.10
  86.6 2.1 %collective-permute-done.10 = bf16[4,16,16,256]{3,2,1,0:T(8,128)(2,1)S(1)} collective-permute-done((bf16[4,16,16,256]{3,2,1,0:T(8,128)(2,1)}, bf16[4,16,16,256]{3,2,1,0:T(8,128)(2,1)S(1)}, u32[]{:S(2)}, u32[]{:S(2)}) %collective-permute-start.10) | collective-permute-done | bytes 524320 | tf_op jit(solution)/shard_map/ppermute | solution.py:403
  88.7 1.2 add_convert_fusion
  90.0 0.1 collective-permute-start.11
  90.1 2.7 %collective-permute-start.13 = (bf16[16,16,256]{2,1,0:T(8,128)(2,1)S(1)}, bf16[16,16,256]{2,1,0:T(8,128)(2,1)S(1)}, u32[]{:S(2)}, u32[]{:S(2)}) collective-permute-start(bf16[16,16,256]{2,1,0:T(8,128)(2,1)S(1)} %get-tuple-element.35), channel_id=1, source_target_pairs={{0,6},{1,7},{2,0},{3,1},{4,2},{5,3},{6,4},{7,5},{8,14},{9,15},{10,... | collective-permute-start | bytes 393224 | tf_op jit(solution)/shard_map/ppermute | solution.py:405
  92.7 0.5 collective-permute-start.12
  93.2 7.8 %tap_grad.1 = bf16[64,256]{1,0:T(8,128)(2,1)} custom-call(bf16[8,256,256]{2,1,0:T(8,128)(2,1)} %bitcast.20, bf16[3,256,256]{2,1,0:T(8,128)(2,1)} %copy-done, bf16[3,256,256]{2,1,0:T(8,128)(2,1)} %copy-done.1, f32[8,256,256]{2,1,0:T(8,128)} %bitcast.21, f32[8,256]{1,0:T(8,128)} %get-tuple-element.28.gsum), custom_call_target="tpu_custom_call" | custom-call | tf_op jit(solution)/shard_map/tap_grad/pallas_call | solution.py:355
  101.1 9.7 %all_to_all.20 = bf16[8,8,256]{2,1,0:T(8,128)(2,1)S(1)} all-to-all(bf16[8,8,256]{2,1,0:T(8,128)(2,1)} %bitcast.22), channel_id=1, replica_groups=mesh['grp'=2,'dp'=16,'row'=8] {'row'}, dimensions={0} | all-to-all | bytes 65536 | tf_op jit(solution)/shard_map/all_to_all | solution.py:412
  110.8 0.0 collective-permute-done.11
  110.8 0.0 collective-permute-done.13
  110.8 0.0 collective-permute-done.12
  110.8 0.1 fusion.2
  111.0 10.1 %all_to_all.21 = bf16[16,24,256]{2,1,0:T(8,128)(2,1)S(1)} all-to-all(bf16[16,24,256]{2,1,0:T(8,128)(2,1)S(1)} %pad_maximum_fusion), channel_id=1, replica_groups=mesh['grp'=2,'dp'=16,'row'=8] {'dp'}, dimensions={0} | all-to-all | bytes 393216 | tf_op jit(solution)/shard_map/all_to_all | solution.py:414
  121.1 11.0 %all_to_all.22.done = bf16[8,24,256]{2,1,0:T(8,128)(2,1)} all-to-all(bf16[8,24,256]{2,1,0:T(8,128)(2,1)S(1)} %broadcast_in_dim.5), channel_id=1, replica_groups=mesh['grp'=2,'dp'=16,'row'=8] {'row'}, dimensions={0} | all-to-all | bytes 196608 | tf_op jit(solution)/shard_map/all_to_all | solution.py:372
  132.1 1.6 %finish.1 = (f32[1,16,1024]{2,1,0:T(8,128)}, f32[1,64,256]{2,1,0:T(8,128)}, f32[7,7,1,256]{3,2,1,0:T(1,128)}, f32[1,256]{1,0:T(1,128)}, f32[1,256]{1,0:T(1,128)}) custom-call(bf16[8,24,256]{2,1,0:T(8,128)(2,1)} %all_to_all.22.done), custom_call_target="tpu_custom_call" | custom-call | tf_op jit(solution)/shard_map/finish/pallas_call | solution.py:83
  (21 shorter events, 0.1 us)
Async XLA Ops:
  3.5 24.0 %all-to-all-start = ((bf16[32,16,256]{2,1,0:T(8,128)(2,1)}), bf16[32,16,256]{2,1,0:T(8,128)(2,1)S(1)}, u32[]{:S(2)}, u32[]{:S(2)}) async-start(bf16[32,16,256]{2,1,0:T(8,128)(2,1)} %get-tuple-element.20), calls=%async_computation | async-start | bytes 524288 | tf_op jit(solution)/shard_map/all_to_all | solution.py:391
  15.6 28.9 %collective-permute-start.7 = (bf16[3,256,256]{2,1,0:T(8,128)(2,1)}, bf16[3,256,256]{2,1,0:T(8,128)(2,1)S(1)}, u32[]{:S(2)}, u32[]{:S(2)}) collective-permute-start(bf16[3,256,256]{2,1,0:T(8,128)(2,1)} %get-tuple-element.21), channel_id=1, source_target_pairs={{0,1},{1,2},{2,3},{3,4},{4,5},{5,6},{6,7},{8,9},{9,10},{10,11},{11... | collective-permute-start | bytes 1179656 | tf_op jit(solution)/shard_map/ppermute | solution.py:388
  27.5 38.6 %copy-start.2 = (bf16[32,16,256]{2,1,0:T(8,128)(2,1)}, bf16[32,16,256]{2,1,0:T(8,128)(2,1)S(1)}, u32[]{:S(2)}) copy-start(bf16[32,16,256]{2,1,0:T(8,128)(2,1)S(1)} %all-to-all-done.refs_0_) | copy-start | bytes 786436
  27.5 17.1 %collective-permute-start.5 = (bf16[32,16,256]{2,1,0:T(8,128)(2,1)S(1)}, bf16[32,16,256]{2,1,0:T(8,128)(2,1)S(1)}, u32[]{:S(2)}, u32[]{:S(2)}) collective-permute-start(bf16[32,16,256]{2,1,0:T(8,128)(2,1)S(1)} %all-to-all-done.refs_0_), channel_id=1, source_target_pairs={{0,6},{1,7},{2,0},{3,1},{4,2},{5,3},{6,4},{7,5},{8,14},{9,15},{10,... | collective-permute-start | bytes 786440 | tf_op jit(solution)/shard_map/ppermute | solution.py:392
  30.0 15.1 %collective-permute-start.3 = (bf16[32,16,256]{2,1,0:T(8,128)(2,1)S(1)}, bf16[32,16,256]{2,1,0:T(8,128)(2,1)S(1)}, u32[]{:S(2)}, u32[]{:S(2)}) collective-permute-start(bf16[32,16,256]{2,1,0:T(8,128)(2,1)S(1)} %all-to-all-done.refs_0_), channel_id=1, source_target_pairs={{0,4},{1,5},{2,6},{3,7},{4,0},{5,1},{6,2},{7,3},{8,12},{9,13},{10,... | collective-permute-start | bytes 786440 | tf_op jit(solution)/shard_map/ppermute | solution.py:392
  30.5 14.7 %collective-permute-start.1 = (bf16[32,16,256]{2,1,0:T(8,128)(2,1)S(1)}, bf16[32,16,256]{2,1,0:T(8,128)(2,1)S(1)}, u32[]{:S(2)}, u32[]{:S(2)}) collective-permute-start(bf16[32,16,256]{2,1,0:T(8,128)(2,1)S(1)} %all-to-all-done.refs_0_), channel_id=1, source_target_pairs={{0,2},{1,3},{2,4},{3,5},{4,6},{5,7},{6,0},{7,1},{8,10},{9,11},{10,... | collective-permute-start | bytes 786440 | tf_op jit(solution)/shard_map/ppermute | solution.py:392
  31.1 6.9 %collective-permute-start.9 = (bf16[64,256]{1,0:T(8,128)(2,1)}, bf16[64,256]{1,0:T(8,128)(2,1)S(1)}, u32[]{:S(2)}, u32[]{:S(2)}) collective-permute-start(bf16[64,256]{1,0:T(8,128)(2,1)} %get-tuple-element.23.own.refs_11_), channel_id=1, source_target_pairs={{0,128},{128,0},{1,129},{129,1},{2,130},{130,2},{3,131},{131,3},{4... | collective-permute-start | bytes 98312 | tf_op jit(solution)/shard_map/ppermute | solution.py:390
  38.0 13.6 %copy-start.3 = (bf16[64,256]{1,0:T(8,128)(2,1)}, bf16[64,256]{1,0:T(8,128)(2,1)S(1)}, u32[]{:S(2)}) copy-start(bf16[64,256]{1,0:T(8,128)(2,1)S(1)} %collective-permute-done.9.men.refs_12_) | copy-start | bytes 98308
  38.0 13.6 %collective-permute-start.8 = (bf16[3,256,256]{2,1,0:T(8,128)(2,1)}, bf16[3,256,256]{2,1,0:T(8,128)(2,1)S(1)}, u32[]{:S(2)}, u32[]{:S(2)}) collective-permute-start(bf16[3,256,256]{2,1,0:T(8,128)(2,1)} %get-tuple-element.22), channel_id=1, source_target_pairs={{1,0},{2,1},{3,2},{4,3},{5,4},{6,5},{7,6},{9,8},{10,9},{11,10},{12... | collective-permute-start | bytes 1179656 | tf_op jit(solution)/shard_map/ppermute | solution.py:389
  44.5 7.1 %copy-start = (bf16[3,256,256]{2,1,0:T(8,128)(2,1)}, bf16[3,256,256]{2,1,0:T(8,128)(2,1)S(1)}, u32[]{:S(2)}) copy-start(bf16[3,256,256]{2,1,0:T(8,128)(2,1)S(1)} %collective-permute-done.7.top) | copy-start | bytes 1179652
  44.5 21.5 %collective-permute-start = (bf16[32,16,256]{2,1,0:T(8,128)(2,1)S(1)}, bf16[32,16,256]{2,1,0:T(8,128)(2,1)S(1)}, u32[]{:S(2)}, u32[]{:S(2)}) collective-permute-start(bf16[32,16,256]{2,1,0:T(8,128)(2,1)S(1)} %all-to-all-done.refs_0_), channel_id=1, source_target_pairs={{0,1},{1,0},{2,3},{3,2},{4,5},{5,4},{6,7},{7,6},{8,9},{9,8},{10,11... | collective-permute-start | bytes 786440 | tf_op jit(solution)/shard_map/ppermute | solution.py:395
  44.7 21.5 %copy-start.4 = (bf16[32,16,256]{2,1,0:T(8,128)(2,1)}, bf16[32,16,256]{2,1,0:T(8,128)(2,1)S(1)}, u32[]{:S(2)}) copy-start(bf16[32,16,256]{2,1,0:T(8,128)(2,1)S(1)} %collective-permute-done.5.refs_6_) | copy-start | bytes 786436
  44.7 21.4 %collective-permute-start.6 = (bf16[32,16,256]{2,1,0:T(8,128)(2,1)S(1)}, bf16[32,16,256]{2,1,0:T(8,128)(2,1)S(1)}, u32[]{:S(2)}, u32[]{:S(2)}) collective-permute-start(bf16[32,16,256]{2,1,0:T(8,128)(2,1)S(1)} %collective-permute-done.5.refs_6_), channel_id=1, source_target_pairs={{0,1},{1,0},{2,3},{3,2},{4,5},{5,4},{6,7},{7,6},{8,9},{9,8},{10,11... | collective-permute-start | bytes 786440 | tf_op jit(solution)/shard_map/ppermute | solution.py:395
  45.1 21.0 %copy-start.5 = (bf16[32,16,256]{2,1,0:T(8,128)(2,1)}, bf16[32,16,256]{2,1,0:T(8,128)(2,1)S(1)}, u32[]{:S(2)}) copy-start(bf16[32,16,256]{2,1,0:T(8,128)(2,1)S(1)} %collective-permute-done.3.refs_4_) | copy-start | bytes 786436
  45.1 20.9 %collective-permute-start.4 = (bf16[32,16,256]{2,1,0:T(8,128)(2,1)S(1)}, bf16[32,16,256]{2,1,0:T(8,128)(2,1)S(1)}, u32[]{:S(2)}, u32[]{:S(2)}) collective-permute-start(bf16[32,16,256]{2,1,0:T(8,128)(2,1)S(1)} %collective-permute-done.3.refs_4_), channel_id=1, source_target_pairs={{0,1},{1,0},{2,3},{3,2},{4,5},{5,4},{6,7},{7,6},{8,9},{9,8},{10,11... | collective-permute-start | bytes 786440 | tf_op jit(solution)/shard_map/ppermute | solution.py:395
  45.3 20.9 %copy-start.6 = (bf16[32,16,256]{2,1,0:T(8,128)(2,1)}, bf16[32,16,256]{2,1,0:T(8,128)(2,1)S(1)}, u32[]{:S(2)}) copy-start(bf16[32,16,256]{2,1,0:T(8,128)(2,1)S(1)} %collective-permute-done.1.refs_2_) | copy-start | bytes 786436
  45.3 20.8 %collective-permute-start.2 = (bf16[32,16,256]{2,1,0:T(8,128)(2,1)S(1)}, bf16[32,16,256]{2,1,0:T(8,128)(2,1)S(1)}, u32[]{:S(2)}, u32[]{:S(2)}) collective-permute-start(bf16[32,16,256]{2,1,0:T(8,128)(2,1)S(1)} %collective-permute-done.1.refs_2_), channel_id=1, source_target_pairs={{0,1},{1,0},{2,3},{3,2},{4,5},{5,4},{6,7},{7,6},{8,9},{9,8},{10,11... | collective-permute-start | bytes 786440 | tf_op jit(solution)/shard_map/ppermute | solution.py:395
  51.6 0.8 copy-start.1
  66.0 0.7 copy-start.7
  66.1 0.8 copy-start.8
  66.1 0.8 copy-start.9
  66.1 0.9 copy-start.10
  86.4 2.4 %collective-permute-start.10 = (bf16[4,16,16,256]{3,2,1,0:T(8,128)(2,1)}, bf16[4,16,16,256]{3,2,1,0:T(8,128)(2,1)S(1)}, u32[]{:S(2)}, u32[]{:S(2)}) collective-permute-start(bf16[4,16,16,256]{3,2,1,0:T(8,128)(2,1)} %get-tuple-element.26), channel_id=1, source_target_pairs={{0,1},{1,0},{2,3},{3,2},{4,5},{5,4},{6,7},{7,6},{8,9},{9,8},{10,11... | collective-permute-start | bytes 1572872 | tf_op jit(solution)/shard_map/ppermute | solution.py:403
  90.0 20.8 %collective-permute-start.11 = (bf16[16,16,256]{2,1,0:T(8,128)(2,1)S(1)}, bf16[16,16,256]{2,1,0:T(8,128)(2,1)S(1)}, u32[]{:S(2)}, u32[]{:S(2)}) collective-permute-start(bf16[16,16,256]{2,1,0:T(8,128)(2,1)S(1)} %get-tuple-element.34), channel_id=1, source_target_pairs={{0,2},{1,3},{2,4},{3,5},{4,6},{5,7},{6,0},{7,1},{8,10},{9,11},{10,... | collective-permute-start | bytes 393224 | tf_op jit(solution)/shard_map/ppermute | solution.py:405
  90.1 20.8 %collective-permute-start.13 = (bf16[16,16,256]{2,1,0:T(8,128)(2,1)S(1)}, bf16[16,16,256]{2,1,0:T(8,128)(2,1)S(1)}, u32[]{:S(2)}, u32[]{:S(2)}) collective-permute-start(bf16[16,16,256]{2,1,0:T(8,128)(2,1)S(1)} %get-tuple-element.35), channel_id=1, source_target_pairs={{0,6},{1,7},{2,0},{3,1},{4,2},{5,3},{6,4},{7,5},{8,14},{9,15},{10,... | collective-permute-start | bytes 393224 | tf_op jit(solution)/shard_map/ppermute | solution.py:405
  92.7 18.1 %collective-permute-start.12 = (bf16[16,16,256]{2,1,0:T(8,128)(2,1)S(1)}, bf16[16,16,256]{2,1,0:T(8,128)(2,1)S(1)}, u32[]{:S(2)}, u32[]{:S(2)}) collective-permute-start(bf16[16,16,256]{2,1,0:T(8,128)(2,1)S(1)} %get-tuple-element.36), channel_id=1, source_target_pairs={{0,4},{1,5},{2,6},{3,7},{4,0},{5,1},{6,2},{7,3},{8,12},{9,13},{10,... | collective-permute-start | bytes 393224 | tf_op jit(solution)/shard_map/ppermute | solution.py:405

commit v2 on v1

--- a/solution.py
+++ b/solution.py
@@ -12,6 +12,8 @@
 INV_SQRT_TAU = 0.3989422804014327
 BF = jnp.bfloat16
 F32 = jnp.float32
+SUB = 512
+TILE = 512
 LEFT = 8
 
 
@@ -171,16 +173,54 @@
     )(img, top, bot, own, men)
 
 
-def pointwise_kernel(*refs, nx, count, inv_count):
+def tap_grad(img, top, bot, up, gsum, pad, lines, taps):
+    rows, cols, chans = img.shape
+    edge = taps // 2
+    fill_padded(pad, img, top, bot, edge)
+    lines[...] = jnp.zeros_like(lines)
+    for cb in range(chans // 128):
+        lanes = slice(cb * 128, cb * 128 + 128)
+        for lo, hi in ((0, 4), (4, taps)):
+
+            def block(wb, accs):
+                accs = list(accs)
+                for u in range(2):
+                    w0 = pl.multiple_of(wb * 32 + u * 16, 16)
+                    ups = [up[h, pl.ds(w0, 16), lanes] for h in range(rows)]
+                    for j in range(lo, hi):
+                        vs = [
+                            pad[cb, r, pl.ds(w0 + (LEFT - edge + j), 16), :].astype(BF)
+                            for r in range(rows + 2 * edge)
+                        ]
+                        for i in range(taps):
+                            term = tree([vs[h + i] * ups[h] for h in range(rows)]).astype(F32)
+                            q = (j - lo) * taps + i
+                            accs[q] = accs[q] + (term[:8] + term[8:])
+                return tuple(accs)
+
+            count = (hi - lo) * taps
+            accs = lax.fori_loop(
+                0, cols // 32, block, tuple(jnp.zeros((8, 128), F32) for _ in range(count))
+            )
+            for q in range(count):
+                tap = (q % taps) * taps + lo + q // taps
+                lines[tap : tap + 1, lanes] = jnp.sum(accs[q], axis=0, keepdims=True)
+        for q in range(2):
+            lines[taps * taps + q : taps * taps + q + 1, lanes] = gsum[q : q + 1, lanes]
+
+
+def pointwise_kernel(*refs, nx, taps, inv_count):
+    count = taps * taps
     bufs = refs[: 2 * nx]
-    (filt_a, filt_b, img, own, men) = refs[2 * nx : 2 * nx + 5]
-    (feat, up_conv, keep, send, gsum) = refs[2 * nx + 5 : 2 * nx + 10]
-    (w_in, w_out, act, slope, g_in, g_out) = refs[2 * nx + 10 :]
+    (filt_a, filt_b, img, top, bot, own, men) = refs[2 * nx : 2 * nx + 7]
+    (feat, keep, send) = refs[2 * nx + 7 : 2 * nx + 10]
+    (w_in, w_out, act, slope, g_in, g_out, normed, up_branch, up_pre, unit_s, up_conv, gsum, pad, lines) = refs[2 * nx + 10 :]
     gain = own[count : count + 1, :].astype(F32)
     s_own = own[count + 1 : count + 2, :].astype(F32)
     s_men = men[count + 1 : count + 2, :].astype(F32)
     step = pl.program_id(0)
-    tile, _ = img.shape
+    _, cols, chans = img.shape
+    tile = feat.shape[0]
     hid = w_out.shape[2]
     dp = bufs[0].shape[0] // 2
     chunks = hid // 256
@@ -212,56 +252,74 @@
         rows = slice(n * 256, n * 256 + 256)
         return jnp.concatenate([w_out[s, 0, rows, :], w_out[s, 1, rows, :]], axis=1)
 
-    branch = [None, None]
-    for s, small in ((0, own), (1, men)):
-        x = jnp.concatenate([filt_a[s].reshape(tile, 128), filt_b[s].reshape(tile, 128)], axis=1)
-        centred = x - jnp.mean(x, axis=-1, keepdims=True)
-        inv = lax.rsqrt(jnp.mean(centred * centred, axis=-1, keepdims=True) + 1e-06)
-        x = centred * inv
-        if s == 0:
-            unit, inv_std = x, inv
-        x = (x * small[count : count + 1, :].astype(F32)).astype(BF)
-        if s == 0:
-            normed_t = x.T
+    per_row = max(1, cols // SUB)
+
+    def block(m, _):
+        at = pl.multiple_of(m * SUB, SUB)
+        line, w0 = (lax.div(m, per_row), pl.multiple_of(lax.rem(m, per_row) * SUB, SUB)) if SUB <= cols else (pl.ds(m * (SUB // cols), SUB // cols), 0)
+        here = pl.ds(at, SUB)
+        branch = [None, None]
+        for s, small in ((0, own), (1, men)):
+            x = jnp.concatenate([f[s, line, pl.ds(w0, min(SUB, cols)), :].reshape(SUB, 128) for f in (filt_a, filt_b)], axis=1)
+            centred = x - jnp.mean(x, axis=-1, keepdims=True)
+            inv = lax.rsqrt(jnp.mean(centred * centred, axis=-1, keepdims=True) + 1e-06)
+            x = centred * inv
+            if s == 0:
+                unit_s[...] = x
+                inv_std = inv
+            x = (x * small[count : count + 1, :].astype(F32)).astype(BF)
+            if s == 0:
+                normed[here, :] = x
+            for n in range(chunks):
+                pre = jnp.dot(x, in_chunk(s, n), preferred_element_type=F32)
+                half_cdf = 0.5 + 0.5 * lax.erf(pre * SQRT_HALF)
+                activated = (pre * half_cdf).astype(BF)
+                if s == 0:
+                    act[here, n * 256 : n * 256 + 256] = activated
+                    slope[:, n * 256 : n * 256 + 256] = (
+                        half_cdf + pre * jnp.exp(-0.5 * pre * pre) * INV_SQRT_TAU
+                    )
+                part = jnp.dot(activated, out_chunk(s, n), preferred_element_type=F32)
+                branch[s] = part if branch[s] is None else branch[s] + part
+        scaled = branch[0] * s_own
+        feat[here, :] = (img[pl.ds(step * (tile // cols), tile // cols)].reshape(tile, chans).astype(F32) + scaled).astype(BF)
+        upstream = (scaled - s_men * branch[1]) * inv_count
+        gsum[1:2, :] = gsum[1:2, :] + jnp.sum(upstream * branch[0], axis=0, keepdims=True)
+        back = (upstream * s_own).astype(BF)
+        up_branch[here, :] = back
+        up_normed = None
         for n in range(chunks):
-            pre = jnp.dot(x, in_chunk(s, n), preferred_element_type=F32)
-            half_cdf = 0.5 + 0.5 * lax.erf(pre * SQRT_HALF)
-            activated = (pre * half_cdf).astype(BF)
-            if s == 0:
-                act[:, n * 256 : n * 256 + 256] = activated
-                slope[:, n * 256 : n * 256 + 256] = (
-                    half_cdf + pre * jnp.exp(-0.5 * pre * pre) * INV_SQRT_TAU
-                )
-            part = jnp.dot(activated, out_chunk(s, n), preferred_element_type=F32)
-            branch[s] = part if branch[s] is None else branch[s] + part
-    scaled = branch[0] * s_own
-    feat[...] = (img[...].astype(F32) + scaled).astype(BF)
-    upstream = (scaled - s_men[...] * branch[1]) * inv_count
-    gsum[1:2, :] = gsum[1:2, :] + jnp.sum(upstream * branch[0], axis=0, keepdims=True)
-    up_branch = (upstream * s_own).astype(BF)
-    up_branch_t = up_branch.T
-    up_normed = None
+            lanes = slice(n * 256, n * 256 + 256)
+            up_active = lax.dot_general(
+                back, out_chunk(0, n), (((1,), (1,)), ((), ())), preferred_element_type=F32
+            )
+            up_p = (up_active * slope[:, lanes]).astype(BF)
+            up_pre[here, lanes] = up_p
+            part = lax.dot_general(
+                up_p, in_chunk(0, n), (((1,), (1,)), ((), ())), preferred_element_type=F32
+            )
+            up_normed = part if up_normed is None else up_normed + part
+        unit = unit_s[...]
+        prod = up_normed * unit
+        gsum[0:1, :] = gsum[0:1, :] + jnp.sum(prod, axis=0, keepdims=True)
+        up_unit = up_normed * gain
+        mean_up = jnp.mean(up_unit, axis=-1, keepdims=True)
+        mean_proj = jnp.mean(prod * gain, axis=-1, keepdims=True)
+        slab = (inv_std * (up_unit - mean_up - unit * mean_proj)).astype(BF)
+        up_conv[pl.ds(step * (tile // cols), tile // cols)] = slab.reshape(tile // cols, cols, chans)
+        return 0
+
+    lax.fori_loop(0, tile // SUB, block, 0)
+    normed_t = normed[...].T
+    up_branch_t = up_branch[...].T
     for n in range(chunks):
-        cols = slice(n * 256, n * 256 + 256)
-        g_out[:, cols] = g_out[:, cols] + jnp.dot(up_branch_t, act[:, cols], preferred_element_type=F32)
-        up_active = lax.dot_general(
-            up_branch, out_chunk(0, n), (((1,), (1,)), ((), ())), preferred_element_type=F32
-        )
-        up_pre = (up_active * slope[:, cols]).astype(BF)
-        g_in[:, cols] = g_in[:, cols] + jnp.dot(normed_t, up_pre, preferred_element_type=F32)
-        part = lax.dot_general(
-            up_pre, in_chunk(0, n), (((1,), (1,)), ((), ())), preferred_element_type=F32
-        )
-        up_normed = part if up_normed is None else up_normed + part
-    prod = up_normed * unit
-    gsum[0:1, :] = gsum[0:1, :] + jnp.sum(prod, axis=0, keepdims=True)
-    up_unit = up_normed * gain
-    mean_up = jnp.mean(up_unit, axis=-1, keepdims=True)
-    mean_proj = jnp.mean(prod * gain, axis=-1, keepdims=True)
-    up_conv[...] = inv_std * (up_unit - mean_up - unit * mean_proj)
+        lanes = slice(n * 256, n * 256 + 256)
+        g_out[:, lanes] = g_out[:, lanes] + jnp.dot(up_branch_t, act[:, lanes], preferred_element_type=F32)
+        g_in[:, lanes] = g_in[:, lanes] + jnp.dot(normed_t, up_pre[:, lanes], preferred_element_type=F32)
 
     @pl.when(step == pl.num_programs(0) - 1)
     def _():
+        tap_grad(img, top, bot, up_conv, gsum, pad, lines, taps)
         g_out_t = g_out[...].astype(BF).T
         for x in range(nx):
             for h in range(2):
@@ -270,97 +328,55 @@
 
                 def emit(out):
                     for d in range(dp):
-                        out[xr, d, :, 0:128] = g_in[d * 16 : d * 16 + 16, lanes].astype(BF)
+                        to = slice(d * 16, d * 16 + 16)
+                        out[xr, to, 0:128] = g_in[to, lanes].astype(BF)
                         lo = d * per_d + 16 * x
-                        out[xr, d, :, 128:256] = g_out_t[lo : lo + 16, 128 * h : 128 * h + 128]
+                        out[xr, to, 128:256] = g_out_t[lo : lo + 16, 128 * h : 128 * h + 128]
+                    r = 2 * x + h
+                    out[xr, dp * 16 : dp * 16 + 8, :] = lines[8 * r : 8 * r + 8, :].astype(BF)
 
                 pl.when(me_c == h)(functools.partial(emit, keep))
                 pl.when(me_c != h)(functools.partial(emit, send))
 
 
-def pointwise(bufs, filt_a, filt_b, img, own, men, hid, count, inv_count):
-    pixels, chans = img.shape
-    _, _, cols, _ = filt_a.shape
+def pointwise(bufs, filt_a, filt_b, img, top, bot, own, men, hid, taps, inv_count):
+    rows, cols, chans = img.shape
+    pixels = rows * cols
     nx = len(bufs) // 2
     dp = bufs[0].shape[0] // 2
-    tile = 512
+    edge = taps // 2
+    tile = TILE
     whole = lambda a: pl.BlockSpec(a.shape, lambda t: (0,) * a.ndim)
-    lines = pl.BlockSpec((tile, chans), lambda t: (t, 0))
     filt = pl.BlockSpec((2, tile // cols, cols, 128), lambda t: (0, t, 0, 0))
-    part = pl.BlockSpec((nx, dp, 16, 256), lambda t: (0, 0, 0, 0))
+    part = pl.BlockSpec((nx, dp * 16 + 8, 256), lambda t: (0, 0, 0))
     return pl.pallas_call(
-        functools.partial(pointwise_kernel, nx=nx, count=count, inv_count=inv_count),
+        functools.partial(pointwise_kernel, nx=nx, taps=taps, inv_count=inv_count),
         out_shape=[
             jax.ShapeDtypeStruct((pixels, chans), BF),
-            jax.ShapeDtypeStruct((pixels, chans), F32),
-            jax.ShapeDtypeStruct((nx, dp, 16, 256), BF),
-            jax.ShapeDtypeStruct((nx, dp, 16, 256), BF),
-            jax.ShapeDtypeStruct((8, chans), F32),
+            jax.ShapeDtypeStruct((nx, dp * 16 + 8, 256), BF),
+            jax.ShapeDtypeStruct((nx, dp * 16 + 8, 256), BF),
         ],
         grid=(pixels // tile,),
-        in_specs=[whole(b) for b in bufs] + [filt, filt, lines, whole(own), whole(men)],
-        out_specs=[lines, lines, part, part, pl.BlockSpec((8, chans), lambda t: (0, 0))],
+        in_specs=[whole(b) for b in bufs] + [filt, filt] + [whole(a) for a in (img, top, bot, own, men)],
+        out_specs=[pl.BlockSpec((tile, chans), lambda t: (t, 0)), part, part],
         scratch_shapes=[
             pltpu.VMEM((2, hid // 128, chans, 128), BF),
             pltpu.VMEM((2, 2, hid, 128), BF),
             pltpu.VMEM((tile, hid), BF),
-            pltpu.VMEM((tile, hid), F32),
+            pltpu.VMEM((SUB, hid), F32),
             pltpu.VMEM((chans, hid), F32),
             pltpu.VMEM((chans, hid), F32),
-        ],
-        name="pointwise",
-    )(*bufs, filt_a, filt_b, img, own, men)
-
-
-def tap_grad_kernel(img, top, bot, up, gsum, out, pad, lines, *, taps):
-    rows, cols, chans = img.shape
-    edge = taps // 2
-    fill_padded(pad, img, top, bot, edge)
-    lines[...] = jnp.zeros_like(lines)
-    for cb in range(chans // 128):
-        lanes = slice(cb * 128, cb * 128 + 128)
-        for lo, hi in ((0, 4), (4, taps)):
-
-            def block(wb, accs):
-                accs = list(accs)
-                for u in range(2):
-                    w0 = pl.multiple_of(wb * 32 + u * 16, 16)
-                    ups = [up[h, pl.ds(w0, 16), lanes].astype(BF) for h in range(rows)]
-                    for j in range(lo, hi):
-                        vs = [
-                            pad[cb, r, pl.ds(w0 + (LEFT - edge + j), 16), :].astype(BF)
-                            for r in range(rows + 2 * edge)
-                        ]
-                        for i in range(taps):
-                            term = tree([vs[h + i] * ups[h] for h in range(rows)]).astype(F32)
-                            q = (j - lo) * taps + i
-                            accs[q] = accs[q] + (term[:8] + term[8:])
-                return tuple(accs)
-
-            count = (hi - lo) * taps
-            accs = lax.fori_loop(
-                0, cols // 32, block, tuple(jnp.zeros((8, 128), F32) for _ in range(count))
-            )
-            for q in range(count):
-                tap = (q % taps) * taps + lo + q // taps
-                lines[tap : tap + 1, lanes] = jnp.sum(accs[q], axis=0, keepdims=True)
-        for q in range(2):
-            lines[taps * taps + q : taps * taps + q + 1, lanes] = gsum[q : q + 1, lanes]
-    out[...] = lines[...].astype(BF)
-
-
-def tap_grad(img, top, bot, up, gsum, taps):
-    rows, cols, chans = img.shape
-    edge = taps // 2
-    return pl.pallas_call(
-        functools.partial(tap_grad_kernel, taps=taps),
-        out_shape=jax.ShapeDtypeStruct((64, chans), BF),
-        scratch_shapes=[
+            pltpu.VMEM((tile, chans), BF),
+            pltpu.VMEM((tile, chans), BF),
+            pltpu.VMEM((tile, hid), BF),
+            pltpu.VMEM((SUB, chans), F32),
+            pltpu.VMEM((rows, cols, chans), BF),
+            pltpu.VMEM((8, chans), F32),
             pltpu.VMEM((chans // 128, rows + 2 * edge, cols + LEFT + 8, 128), F32),
             pltpu.VMEM((64, chans), F32),
         ],
-        name="tap_grad",
-    )(img, top, bot, up, gsum)
+        name="pointwise",
+    )(*bufs, filt_a, filt_b, img, top, bot, own, men)
 
 
 def total(block):
@@ -374,9 +390,8 @@
 
 def step(images, w_in, w_out, kernel, gain, scale):
     pictures = images[0, 0]
-    row_count, col_count, channels = pictures.shape
+    row_count, col_count, _ = pictures.shape
     taps = kernel.shape[1]
-    count = taps * taps
     dp, row, grp = lax.axis_size("dp"), lax.axis_size("row"), lax.axis_size("grp")
     nx = row // 2
     hid = w_in.shape[2]
@@ -396,8 +411,8 @@
 
     filt_a = conv(pictures, top, bot, small, men_small, taps, 0)
     filt_b = conv(pictures, top, bot, small, men_small, taps, 1)
-    feat, up_conv, keep, send, gsum = pointwise(
-        bufs, filt_a, filt_b, pictures.reshape(-1, channels), small, men_small, hid, count, inv_count
+    feat, keep, send = pointwise(
+        bufs, filt_a, filt_b, pictures, top, bot, small, men_small, hid, taps, inv_count
     )
     wide = lambda a: a.astype(F32)
     other = lax.ppermute(send, "row", twin)
@@ -407,9 +422,8 @@
     for block in sent:
         line_sum = line_sum + wide(block)
     line_sum = line_sum.astype(BF)
-    rest = tap_grad(pictures, top, bot, up_conv.reshape(row_count, col_count, channels), gsum, taps)
-    rest = rest.reshape(row, 64 // row, channels)
-    rest = total(lax.all_to_all(rest, "row", 0, 0, tiled=True)).astype(BF)
+    rest = line_sum[dp * 16 :]
+    line_sum = line_sum[: dp * 16].reshape(dp, 16, 256)
     rest = jnp.broadcast_to(rest[None], (dp,) + rest.shape)
     piece_sum = total(lax.all_to_all(jnp.concatenate([line_sum, rest], axis=1), "dp", 0, 0, tiled=True))
     grad_in, grad_out, grad_kern, *rest = finish(spread(piece_sum.astype(BF), "row"), taps)

time: 134 us -> 127 us (0.948)
  blocking collectives: 30.8 us -> 22.4 us
  waiting for transfers between devices: 21.3 us -> 26.7 us
  Pallas kernels: 45.3 us -> 40.6 us
    all_to_all x1 -> x0, blocking collectives: 9.69 us -> none  [step(): rest = total(lax.all_to_all(rest, 'row', 0, 0, tiled=True)).astype(BF)]
    ppermute x3, waiting for transfers between devices: 0.01 us -> 5.42 us  [step(): sent = [lax.ppermute(chip[k], 'row', chips(k)) for k in range(1, nx)]]
    pallas_call x2 -> x1, Pallas kernels: 27.2 us -> 22.4 us  [pointwise(): pl.pallas_call(functools.partial(pointwise_kernel, nx=nx, taps=taps, inv_...]
  transfers between devices with their start and end apart: 15 -> 15, of which waited for: 4 -> 7; matrix products, arithmetic and copies ran while one was open for 0% -> 0% of each run, Pallas kernels for 16% -> 11%
where the time goes in v2:
time: 127 us
  Pallas kernels  40.6 us (32%)
  starting transfers between devices  32.4 us (26%)
  waiting for transfers between devices  26.7 us (21%)
  blocking collectives  22.4 us (18%)
  local copies, waits for them, and re-layouts  2.41 us (2%)
  other arithmetic  1.31 us (1%)
    pallas_call x1, Pallas kernels, pointwise(): pl.pallas_call(functools.partial(pointwise_kernel, nx=nx, taps=taps, inv_...  22.4 us
    pallas_call x2, Pallas kernels, conv(): pl.pallas_call(functools.partial(conv_kernel, taps=taps), out_shape=jax.S...  13.7 us
    all_to_all x1, blocking collectives, spread(): return lax.all_to_all(copies, axis, 0, 0, tiled=True)  12.3 us
    all_to_all x1, starting transfers between devices, step(): line = lax.all_to_all(piece, ('grp', 'dp'), 0, 0, tiled=True)  12 us
    all_to_all x1, blocking collectives, step(): lax.all_to_all(jnp.concatenate([line_sum, rest], axis=1), 'dp', 0, 0, til...  10.1 us
    all_to_all x1, waiting for transfers between devices, step(): line = lax.all_to_all(piece, ('grp', 'dp'), 0, 0, tiled=True)  8 us
    ppermute x1, starting transfers between devices, step(): bot = lax.ppermute(head, 'row', [(i + 1, i) for i in range(row - 1)])  6.48 us
    ppermute x1, waiting for transfers between devices, step(): bot = lax.ppermute(head, 'row', [(i + 1, i) for i in range(row - 1)])  5.72 us
  transfers between devices with their start and end apart: 15, of which 7 were waited for; matrix products, arithmetic and copies ran while one was open for 0% of the time, Pallas kernels for 11%

profile of v2, /device:TPU:1, one launch (start us, length us, event | category | flops | bytes accessed | tf_op | source)
XLA Modules:
  0.0 126.7 jit_solution(16408326669750918879)
XLA Ops:
  0.6 2.9 %prep.1 = (bf16[3,256,256]{2,1,0:T(8,128)(2,1)}, bf16[3,256,256]{2,1,0:T(8,128)(2,1)}, bf16[32,16,256]{2,1,0:T(8,128)(2,1)}, bf16[64,256]{1,0:T(8,128)(2,1)}) custom-call(bf16[1,1,8,256,256]{4,3,2,1,0:T(8,128)(2,1)} %images.1, bf16[1,16,1024]{2,1,0:T(8,128)(2,1)} %w_in.1, bf16[1,64,256]{2,1,0:T(8,128)(2,1)} %w_out.1, bf16[1,7,7,256]{3,2,1,0:T(8,128)(2,1)} %kernel.1, ...), custom_call_target="tpu_custom_call" | custom-call | tf_op jit(solution)/shard_map/prep/pallas_call | solution.py:54
  3.5 12.0 %all-to-all-start = ((bf16[32,16,256]{2,1,0:T(8,128)(2,1)}), bf16[32,16,256]{2,1,0:T(8,128)(2,1)S(1)}, u32[]{:S(2)}, u32[]{:S(2)}) async-start(bf16[32,16,256]{2,1,0:T(8,128)(2,1)} %get-tuple-element.18), calls=%async_computation | async-start | bytes 524288 | tf_op jit(solution)/shard_map/all_to_all | solution.py:406
  15.6 4.0 %collective-permute-start.7 = (bf16[3,256,256]{2,1,0:T(8,128)(2,1)}, bf16[3,256,256]{2,1,0:T(8,128)(2,1)S(1)}, u32[]{:S(2)}, u32[]{:S(2)}) collective-permute-start(bf16[3,256,256]{2,1,0:T(8,128)(2,1)} %get-tuple-element.19), channel_id=1, source_target_pairs={{0,1},{1,2},{2,3},{3,4},{4,5},{5,6},{6,7},{8,9},{9,10},{10,11},{11... | collective-permute-start | bytes 1179656 | tf_op jit(solution)/shard_map/ppermute | solution.py:403
  19.5 8.0 %all-to-all-done.refs_0_ = bf16[32,16,256]{2,1,0:T(8,128)(2,1)S(1)} async-done(((bf16[32,16,256]{2,1,0:T(8,128)(2,1)}), bf16[32,16,256]{2,1,0:T(8,128)(2,1)S(1)}, u32[]{:S(2)}, u32[]{:S(2)}) %all-to-all-start) | async-done | bytes 262176 | tf_op jit(solution)/shard_map/all_to_all | solution.py:406
  27.5 2.5 %collective-permute-start.5 = (bf16[32,16,256]{2,1,0:T(8,128)(2,1)S(1)}, bf16[32,16,256]{2,1,0:T(8,128)(2,1)S(1)}, u32[]{:S(2)}, u32[]{:S(2)}) collective-permute-start(bf16[32,16,256]{2,1,0:T(8,128)(2,1)S(1)} %all-to-all-done.refs_0_), channel_id=1, source_target_pairs={{0,6},{1,7},{2,0},{3,1},{4,2},{5,3},{6,4},{7,5},{8,14},{9,15},{10,... | collective-permute-start | bytes 786440 | tf_op jit(solution)/shard_map/ppermute | solution.py:407
  30.0 0.5 collective-permute-start.3
  30.5 0.6 collective-permute-start.1
  31.2 1.5 %collective-permute-start.9 = (bf16[64,256]{1,0:T(8,128)(2,1)}, bf16[64,256]{1,0:T(8,128)(2,1)S(1)}, u32[]{:S(2)}, u32[]{:S(2)}) collective-permute-start(bf16[64,256]{1,0:T(8,128)(2,1)} %get-tuple-element.21.own.refs_13_), channel_id=1, source_target_pairs={{0,128},{128,0},{1,129},{129,1},{2,130},{130,2},{3,131},{131,3},{4... | collective-permute-start | bytes 98312 | tf_op jit(solution)/shard_map/ppermute | solution.py:405
  32.6 5.4 %collective-permute-done.9.men.refs_14_ = bf16[64,256]{1,0:T(8,128)(2,1)S(1)} collective-permute-done((bf16[64,256]{1,0:T(8,128)(2,1)}, bf16[64,256]{1,0:T(8,128)(2,1)S(1)}, u32[]{:S(2)}, u32[]{:S(2)}) %collective-permute-start.9) | collective-permute-done | bytes 32800 | tf_op jit(solution)/shard_map/ppermute | solution.py:405
  38.0 6.5 %collective-permute-start.8 = (bf16[3,256,256]{2,1,0:T(8,128)(2,1)}, bf16[3,256,256]{2,1,0:T(8,128)(2,1)S(1)}, u32[]{:S(2)}, u32[]{:S(2)}) collective-permute-start(bf16[3,256,256]{2,1,0:T(8,128)(2,1)} %get-tuple-element.20), channel_id=1, source_target_pairs={{1,0},{2,1},{3,2},{4,3},{5,4},{6,5},{7,6},{9,8},{10,9},{11,10},{12... | collective-permute-start | bytes 1179656 | tf_op jit(solution)/shard_map/ppermute | solution.py:404
  44.5 0.0 collective-permute-done.7.top.refs_11_
  44.5 0.0 copy-start
  44.5 0.1 collective-permute-start
  44.6 0.0 collective-permute-done.5.refs_6_
  44.7 0.0 copy-start.4
  44.7 0.5 collective-permute-start.6
  45.1 0.0 collective-permute-done.3.refs_4_
  45.2 0.1 collective-permute-start.4
  45.3 0.0 collective-permute-done.1.refs_2_
  45.3 0.6 collective-permute-start.2
  45.9 5.7 %collective-permute-done.8.bot.refs_12_ = bf16[3,256,256]{2,1,0:T(8,128)(2,1)S(1)} collective-permute-done((bf16[3,256,256]{2,1,0:T(8,128)(2,1)}, bf16[3,256,256]{2,1,0:T(8,128)(2,1)S(1)}, u32[]{:S(2)}, u32[]{:S(2)}) %collective-permute-start.8) | collective-permute-done | bytes 393248 | tf_op jit(solution)/shard_map/ppermute | solution.py:404
  51.6 0.8 copy-done.1
  52.4 6.8 %shard_map.110.refs_9_ = f32[2,8,256,128]{3,2,1,0:T(8,128)} custom-call(bf16[8,256,256]{2,1,0:T(8,128)(2,1)} %bitcast.15, bf16[3,256,256]{2,1,0:T(8,128)(2,1)} %copy-done, bf16[3,256,256]{2,1,0:T(8,128)(2,1)} %copy-done.1, bf16[64,256]{1,0:T(8,128)(2,1)} %get-tuple-element.21.own.refs_13_, bf16[64,256]{1,0:T(8,128)(2,1)} %copy-done.3), custom_call_target="tpu_custom_call" | custom-call | tf_op jit(solution)/shard_map/pallas_call | solution.py:163
  59.2 6.9 %shard_map.109.refs_8_ = f32[2,8,256,128]{3,2,1,0:T(8,128)} custom-call(bf16[8,256,256]{2,1,0:T(8,128)(2,1)} %bitcast.16, bf16[3,256,256]{2,1,0:T(8,128)(2,1)} %copy-done, bf16[3,256,256]{2,1,0:T(8,128)(2,1)} %copy-done.1, bf16[64,256]{1,0:T(8,128)(2,1)} %get-tuple-element.21.own.refs_13_, bf16[64,256]{1,0:T(8,128)(2,1)} %copy-done.3), custom_call_target="tpu_custom_call" | custom-call | tf_op jit(solution)/shard_map/pallas_call | solution.py:163
  66.1 0.0 copy-done.4
  66.1 0.0 collective-permute-done.refs_1_
  66.1 0.0 copy-start.7
  66.1 0.0 collective-permute-done.6.refs_7_
  66.2 0.0 collective-permute-done.4.refs_5_
  66.2 0.0 collective-permute-done.2.refs_3_
  66.2 0.6 copy-done.7
  66.8 0.1 copy-done.8
  66.9 0.1 copy-done.9
  67.0 0.7 copy-done.10
  67.8 22.4 %pointwise.1 = (bf16[2048,256]{1,0:T(8,128)(2,1)}, bf16[4,264,256]{2,1,0:T(8,128)(2,1)}, bf16[4,264,256]{2,1,0:T(8,128)(2,1)}) custom-call(bf16[32,16,256]{2,1,0:T(8,128)(2,1)} %copy-done.2, bf16[32,16,256]{2,1,0:T(8,128)(2,1)} %copy-done.7, bf16[32,16,256]{2,1,0:T(8,128)(2,1)} %copy-done.6, bf16[32,16,256]{2,1,0:T(8,128)(2,1)} %copy-done.10, ...), custom_call_target="tpu_custom_call" | custom-call | tf_op jit(solution)/shard_map/pointwise/pallas_call | solution.py:352
  90.2 0.3 collective-permute-start.10
  90.5 2.1 %collective-permute-done.10 = bf16[4,264,256]{2,1,0:T(8,128)(2,1)S(1)} collective-permute-done((bf16[4,264,256]{2,1,0:T(8,128)(2,1)}, bf16[4,264,256]{2,1,0:T(8,128)(2,1)S(1)}, u32[]{:S(2)}, u32[]{:S(2)}) %collective-permute-start.10) | collective-permute-done | bytes 540704 | tf_op jit(solution)/shard_map/ppermute | solution.py:418
  92.6 1.2 add_convert_fusion
  93.8 0.1 collective-permute-start.11
  93.9 2.7 %collective-permute-start.13 = (bf16[264,256]{1,0:T(8,128)(2,1)S(1)}, bf16[264,256]{1,0:T(8,128)(2,1)S(1)}, u32[]{:S(2)}, u32[]{:S(2)}) collective-permute-start(bf16[264,256]{1,0:T(8,128)(2,1)S(1)} %get-tuple-element.31), channel_id=1, source_target_pairs={{0,6},{1,7},{2,0},{3,1},{4,2},{5,3},{6,4},{7,5},{8,14},{9,15},{10,... | collective-permute-start | bytes 405512 | tf_op jit(solution)/shard_map/ppermute | solution.py:420
  96.6 0.5 collective-permute-start.12
  97.1 3.0 %collective-permute-done.11 = bf16[264,256]{1,0:T(8,128)(2,1)S(1)} collective-permute-done((bf16[264,256]{1,0:T(8,128)(2,1)S(1)}, bf16[264,256]{1,0:T(8,128)(2,1)S(1)}, u32[]{:S(2)}, u32[]{:S(2)}) %collective-permute-start.11) | collective-permute-done | bytes 135200 | tf_op jit(solution)/shard_map/ppermute | solution.py:420
  100.1 1.8 %collective-permute-done.13 = bf16[264,256]{1,0:T(8,128)(2,1)S(1)} collective-permute-done((bf16[264,256]{1,0:T(8,128)(2,1)S(1)}, bf16[264,256]{1,0:T(8,128)(2,1)S(1)}, u32[]{:S(2)}, u32[]{:S(2)}) %collective-permute-start.13) | collective-permute-done | bytes 135200 | tf_op jit(solution)/shard_map/ppermute | solution.py:420
  101.9 0.6 collective-permute-done.12
  102.5 0.1 fusion.2
  102.7 10.1 %all_to_all.15 = bf16[16,24,256]{2,1,0:T(8,128)(2,1)S(1)} all-to-all(bf16[16,24,256]{2,1,0:T(8,128)(2,1)S(1)} %pad_maximum_fusion), channel_id=1, replica_groups=mesh['grp'=2,'dp'=16,'row'=8] {'dp'}, dimensions={0} | all-to-all | bytes 393216 | tf_op jit(solution)/shard_map/all_to_all | solution.py:428
  112.9 12.3 %all_to_all.16.done = bf16[8,24,256]{2,1,0:T(8,128)(2,1)} all-to-all(bf16[8,24,256]{2,1,0:T(8,128)(2,1)S(1)} %broadcast_in_dim.5), channel_id=1, replica_groups=mesh['grp'=2,'dp'=16,'row'=8] {'row'}, dimensions={0} | all-to-all | bytes 196608 | tf_op jit(solution)/shard_map/all_to_all | solution.py:388
  125.1 1.6 %finish.1 = (f32[1,16,1024]{2,1,0:T(8,128)}, f32[1,64,256]{2,1,0:T(8,128)}, f32[7,7,1,256]{3,2,1,0:T(1,128)}, f32[1,256]{1,0:T(1,128)}, f32[1,256]{1,0:T(1,128)}) custom-call(bf16[8,24,256]{2,1,0:T(8,128)(2,1)} %all_to_all.16.done), custom_call_target="tpu_custom_call" | custom-call | tf_op jit(solution)/shard_map/finish/pallas_call | solution.py:85
  (20 shorter events, 0.1 us)
Async XLA Ops:
  3.5 24.0 %all-to-all-start = ((bf16[32,16,256]{2,1,0:T(8,128)(2,1)}), bf16[32,16,256]{2,1,0:T(8,128)(2,1)S(1)}, u32[]{:S(2)}, u32[]{:S(2)}) async-start(bf16[32,16,256]{2,1,0:T(8,128)(2,1)} %get-tuple-element.18), calls=%async_computation | async-start | bytes 524288 | tf_op jit(solution)/shard_map/all_to_all | solution.py:406
  15.6 28.9 %collective-permute-start.7 = (bf16[3,256,256]{2,1,0:T(8,128)(2,1)}, bf16[3,256,256]{2,1,0:T(8,128)(2,1)S(1)}, u32[]{:S(2)}, u32[]{:S(2)}) collective-permute-start(bf16[3,256,256]{2,1,0:T(8,128)(2,1)} %get-tuple-element.19), channel_id=1, source_target_pairs={{0,1},{1,2},{2,3},{3,4},{4,5},{5,6},{6,7},{8,9},{9,10},{10,11},{11... | collective-permute-start | bytes 1179656 | tf_op jit(solution)/shard_map/ppermute | solution.py:403
  27.5 38.6 %copy-start.2 = (bf16[32,16,256]{2,1,0:T(8,128)(2,1)}, bf16[32,16,256]{2,1,0:T(8,128)(2,1)S(1)}, u32[]{:S(2)}) copy-start(bf16[32,16,256]{2,1,0:T(8,128)(2,1)S(1)} %all-to-all-done.refs_0_) | copy-start | bytes 786436
  27.5 17.1 %collective-permute-start.5 = (bf16[32,16,256]{2,1,0:T(8,128)(2,1)S(1)}, bf16[32,16,256]{2,1,0:T(8,128)(2,1)S(1)}, u32[]{:S(2)}, u32[]{:S(2)}) collective-permute-start(bf16[32,16,256]{2,1,0:T(8,128)(2,1)S(1)} %all-to-all-done.refs_0_), channel_id=1, source_target_pairs={{0,6},{1,7},{2,0},{3,1},{4,2},{5,3},{6,4},{7,5},{8,14},{9,15},{10,... | collective-permute-start | bytes 786440 | tf_op jit(solution)/shard_map/ppermute | solution.py:407
  30.0 15.1 %collective-permute-start.3 = (bf16[32,16,256]{2,1,0:T(8,128)(2,1)S(1)}, bf16[32,16,256]{2,1,0:T(8,128)(2,1)S(1)}, u32[]{:S(2)}, u32[]{:S(2)}) collective-permute-start(bf16[32,16,256]{2,1,0:T(8,128)(2,1)S(1)} %all-to-all-done.refs_0_), channel_id=1, source_target_pairs={{0,4},{1,5},{2,6},{3,7},{4,0},{5,1},{6,2},{7,3},{8,12},{9,13},{10,... | collective-permute-start | bytes 786440 | tf_op jit(solution)/shard_map/ppermute | solution.py:407
  30.5 14.7 %collective-permute-start.1 = (bf16[32,16,256]{2,1,0:T(8,128)(2,1)S(1)}, bf16[32,16,256]{2,1,0:T(8,128)(2,1)S(1)}, u32[]{:S(2)}, u32[]{:S(2)}) collective-permute-start(bf16[32,16,256]{2,1,0:T(8,128)(2,1)S(1)} %all-to-all-done.refs_0_), channel_id=1, source_target_pairs={{0,2},{1,3},{2,4},{3,5},{4,6},{5,7},{6,0},{7,1},{8,10},{9,11},{10,... | collective-permute-start | bytes 786440 | tf_op jit(solution)/shard_map/ppermute | solution.py:407
  31.2 6.9 %collective-permute-start.9 = (bf16[64,256]{1,0:T(8,128)(2,1)}, bf16[64,256]{1,0:T(8,128)(2,1)S(1)}, u32[]{:S(2)}, u32[]{:S(2)}) collective-permute-start(bf16[64,256]{1,0:T(8,128)(2,1)} %get-tuple-element.21.own.refs_13_), channel_id=1, source_target_pairs={{0,128},{128,0},{1,129},{129,1},{2,130},{130,2},{3,131},{131,3},{4... | collective-permute-start | bytes 98312 | tf_op jit(solution)/shard_map/ppermute | solution.py:405
  38.0 13.6 %copy-start.3 = (bf16[64,256]{1,0:T(8,128)(2,1)}, bf16[64,256]{1,0:T(8,128)(2,1)S(1)}, u32[]{:S(2)}) copy-start(bf16[64,256]{1,0:T(8,128)(2,1)S(1)} %collective-permute-done.9.men.refs_14_) | copy-start | bytes 98308
  38.0 13.6 %collective-permute-start.8 = (bf16[3,256,256]{2,1,0:T(8,128)(2,1)}, bf16[3,256,256]{2,1,0:T(8,128)(2,1)S(1)}, u32[]{:S(2)}, u32[]{:S(2)}) collective-permute-start(bf16[3,256,256]{2,1,0:T(8,128)(2,1)} %get-tuple-element.20), channel_id=1, source_target_pairs={{1,0},{2,1},{3,2},{4,3},{5,4},{6,5},{7,6},{9,8},{10,9},{11,10},{12... | collective-permute-start | bytes 1179656 | tf_op jit(solution)/shard_map/ppermute | solution.py:404
  44.5 7.1 %copy-start = (bf16[3,256,256]{2,1,0:T(8,128)(2,1)}, bf16[3,256,256]{2,1,0:T(8,128)(2,1)S(1)}, u32[]{:S(2)}) copy-start(bf16[3,256,256]{2,1,0:T(8,128)(2,1)S(1)} %collective-permute-done.7.top.refs_11_) | copy-start | bytes 1179652
  44.5 21.6 %collective-permute-start = (bf16[32,16,256]{2,1,0:T(8,128)(2,1)S(1)}, bf16[32,16,256]{2,1,0:T(8,128)(2,1)S(1)}, u32[]{:S(2)}, u32[]{:S(2)}) collective-permute-start(bf16[32,16,256]{2,1,0:T(8,128)(2,1)S(1)} %all-to-all-done.refs_0_), channel_id=1, source_target_pairs={{0,1},{1,0},{2,3},{3,2},{4,5},{5,4},{6,7},{7,6},{8,9},{9,8},{10,11... | collective-permute-start | bytes 786440 | tf_op jit(solution)/shard_map/ppermute | solution.py:410
  44.7 21.4 %copy-start.4 = (bf16[32,16,256]{2,1,0:T(8,128)(2,1)}, bf16[32,16,256]{2,1,0:T(8,128)(2,1)S(1)}, u32[]{:S(2)}) copy-start(bf16[32,16,256]{2,1,0:T(8,128)(2,1)S(1)} %collective-permute-done.5.refs_6_) | copy-start | bytes 786436
  44.7 21.5 %collective-permute-start.6 = (bf16[32,16,256]{2,1,0:T(8,128)(2,1)S(1)}, bf16[32,16,256]{2,1,0:T(8,128)(2,1)S(1)}, u32[]{:S(2)}, u32[]{:S(2)}) collective-permute-start(bf16[32,16,256]{2,1,0:T(8,128)(2,1)S(1)} %collective-permute-done.5.refs_6_), channel_id=1, source_target_pairs={{0,1},{1,0},{2,3},{3,2},{4,5},{5,4},{6,7},{7,6},{8,9},{9,8},{10,11... | collective-permute-start | bytes 786440 | tf_op jit(solution)/shard_map/ppermute | solution.py:410
  45.1 21.0 %copy-start.5 = (bf16[32,16,256]{2,1,0:T(8,128)(2,1)}, bf16[32,16,256]{2,1,0:T(8,128)(2,1)S(1)}, u32[]{:S(2)}) copy-start(bf16[32,16,256]{2,1,0:T(8,128)(2,1)S(1)} %collective-permute-done.3.refs_4_) | copy-start | bytes 786436
  45.2 21.0 %collective-permute-start.4 = (bf16[32,16,256]{2,1,0:T(8,128)(2,1)S(1)}, bf16[32,16,256]{2,1,0:T(8,128)(2,1)S(1)}, u32[]{:S(2)}, u32[]{:S(2)}) collective-permute-start(bf16[32,16,256]{2,1,0:T(8,128)(2,1)S(1)} %collective-permute-done.3.refs_4_), channel_id=1, source_target_pairs={{0,1},{1,0},{2,3},{3,2},{4,5},{5,4},{6,7},{7,6},{8,9},{9,8},{10,11... | collective-permute-start | bytes 786440 | tf_op jit(solution)/shard_map/ppermute | solution.py:410
  45.3 20.8 %copy-start.6 = (bf16[32,16,256]{2,1,0:T(8,128)(2,1)}, bf16[32,16,256]{2,1,0:T(8,128)(2,1)S(1)}, u32[]{:S(2)}) copy-start(bf16[32,16,256]{2,1,0:T(8,128)(2,1)S(1)} %collective-permute-done.1.refs_2_) | copy-start | bytes 786436
  45.3 20.9 %collective-permute-start.2 = (bf16[32,16,256]{2,1,0:T(8,128)(2,1)S(1)}, bf16[32,16,256]{2,1,0:T(8,128)(2,1)S(1)}, u32[]{:S(2)}, u32[]{:S(2)}) collective-permute-start(bf16[32,16,256]{2,1,0:T(8,128)(2,1)S(1)} %collective-permute-done.1.refs_2_), channel_id=1, source_target_pairs={{0,1},{1,0},{2,3},{3,2},{4,5},{5,4},{6,7},{7,6},{8,9},{9,8},{10,11... | collective-permute-start | bytes 786440 | tf_op jit(solution)/shard_map/ppermute | solution.py:410
  51.6 0.8 copy-start.1
  66.1 0.7 copy-start.7
  66.1 0.8 copy-start.8
  66.2 0.9 copy-start.9
  67.0 0.7 copy-start.10
  90.2 2.4 %collective-permute-start.10 = (bf16[4,264,256]{2,1,0:T(8,128)(2,1)}, bf16[4,264,256]{2,1,0:T(8,128)(2,1)S(1)}, u32[]{:S(2)}, u32[]{:S(2)}) collective-permute-start(bf16[4,264,256]{2,1,0:T(8,128)(2,1)} %get-tuple-element.24), channel_id=1, source_target_pairs={{0,1},{1,0},{2,3},{3,2},{4,5},{5,4},{6,7},{7,6},{8,9},{9,8},{10,11... | collective-permute-start | bytes 1622024 | tf_op jit(solution)/shard_map/ppermute | solution.py:418
  93.8 6.3 %collective-permute-start.11 = (bf16[264,256]{1,0:T(8,128)(2,1)S(1)}, bf16[264,256]{1,0:T(8,128)(2,1)S(1)}, u32[]{:S(2)}, u32[]{:S(2)}) collective-permute-start(bf16[264,256]{1,0:T(8,128)(2,1)S(1)} %get-tuple-element.30), channel_id=1, source_target_pairs={{0,2},{1,3},{2,4},{3,5},{4,6},{5,7},{6,0},{7,1},{8,10},{9,11},{10,... | collective-permute-start | bytes 405512 | tf_op jit(solution)/shard_map/ppermute | solution.py:420
  93.9 8.0 %collective-permute-start.13 = (bf16[264,256]{1,0:T(8,128)(2,1)S(1)}, bf16[264,256]{1,0:T(8,128)(2,1)S(1)}, u32[]{:S(2)}, u32[]{:S(2)}) collective-permute-start(bf16[264,256]{1,0:T(8,128)(2,1)S(1)} %get-tuple-element.31), channel_id=1, source_target_pairs={{0,6},{1,7},{2,0},{3,1},{4,2},{5,3},{6,4},{7,5},{8,14},{9,15},{10,... | collective-permute-start | bytes 405512 | tf_op jit(solution)/shard_map/ppermute | solution.py:420
  96.6 6.0 %collective-permute-start.12 = (bf16[264,256]{1,0:T(8,128)(2,1)S(1)}, bf16[264,256]{1,0:T(8,128)(2,1)S(1)}, u32[]{:S(2)}, u32[]{:S(2)}) collective-permute-start(bf16[264,256]{1,0:T(8,128)(2,1)S(1)} %get-tuple-element.32), channel_id=1, source_target_pairs={{0,4},{1,5},{2,6},{3,7},{4,0},{5,1},{6,2},{7,3},{8,12},{9,13},{10,... | collective-permute-start | bytes 405512 | tf_op jit(solution)/shard_map/ppermute | solution.py:420

commit v3 on v2

--- a/solution.py
+++ b/solution.py
@@ -22,12 +22,28 @@
     return [(i, (i + shift) % count) for i in range(count)]
 
 
-def prep_kernel(images, w_in, w_out, kernel, gain, scale, head, tail, piece, small, lines, sems, *, edge):
-    rows = images.shape[2]
+def edges_kernel(images, head, tail, sems):
+    rows, edge = images.shape[2], head.shape[0]
     up = pltpu.make_async_copy(images.at[0, 0, pl.ds(0, edge)], head, sems.at[0])
     down = pltpu.make_async_copy(images.at[0, 0, pl.ds(rows - edge, edge)], tail, sems.at[1])
     up.start()
     down.start()
+    up.wait()
+    down.wait()
+
+
+def edges(images, edge):
+    out = jax.ShapeDtypeStruct((edge,) + images.shape[3:], BF)
+    return pl.pallas_call(
+        edges_kernel,
+        out_shape=[out, out],
+        in_specs=[pl.BlockSpec(memory_space=pl.ANY)],
+        scratch_shapes=[pltpu.SemaphoreType.DMA((2,))],
+        name="edges",
+    )(images)
+
+
+def prep_kernel(w_in, w_out, kernel, gain, scale, piece, small, lines):
     me = lax.axis_index("row")
     me_x, me_c = lax.div(me, 2), lax.rem(me, 2)
     part_in = w_in[0, :, pl.ds(pl.multiple_of(128 * me, 128), 128)]
@@ -42,28 +58,19 @@
     lines[taps * taps : taps * taps + 1, :] = gain[...].astype(F32)
     lines[taps * taps + 1 : taps * taps + 2, :] = scale[...].astype(F32)
     small[...] = lines[...].astype(BF)
-    up.wait()
-    down.wait()
-
-
-def prep(images, w_in, w_out, kernel, gain, scale, copies):
-    cols, chans = images.shape[3:]
-    edge = kernel.shape[1] // 2
-    anywhere = pl.BlockSpec(memory_space=pl.ANY)
-    vmem = pl.BlockSpec(memory_space=pltpu.VMEM)
+
+
+def prep(w_in, w_out, kernel, gain, scale, copies):
+    chans = gain.shape[1]
     return pl.pallas_call(
-        functools.partial(prep_kernel, edge=edge),
+        prep_kernel,
         out_shape=[
-            jax.ShapeDtypeStruct((edge, cols, chans), BF),
-            jax.ShapeDtypeStruct((edge, cols, chans), BF),
             jax.ShapeDtypeStruct((copies, 16, 256), BF),
             jax.ShapeDtypeStruct((64, chans), BF),
         ],
-        in_specs=[anywhere] + [vmem] * 5,
-        out_specs=[vmem] * 4,
-        scratch_shapes=[pltpu.VMEM((64, chans), F32), pltpu.SemaphoreType.DMA((2,))],
+        scratch_shapes=[pltpu.VMEM((64, chans), F32)],
         name="prep",
-    )(images, w_in, w_out, kernel, gain, scale)
+    )(w_in, w_out, kernel, gain, scale)
 
 
 def finish_kernel(done, grad_in, grad_out, grad_kern, grad_gain, grad_scale, lines):
@@ -399,7 +406,8 @@
     twin = [(i, i ^ 1) for i in range(row)]
     chips = lambda k: [(i, (i + 2 * k) % row) for i in range(row)]
 
-    head, tail, piece, small = prep(images, w_in, w_out, kernel, gain, scale, grp * dp)
+    piece, small = prep(w_in, w_out, kernel, gain, scale, grp * dp)
+    head, tail = edges(images, taps // 2)
     top = lax.ppermute(tail, "row", [(i, i + 1) for i in range(row - 1)])
     bot = lax.ppermute(head, "row", [(i + 1, i) for i in range(row - 1)])
     men_small = lax.ppermute(small, "grp", ring("grp", 1))

time: 127 us -> 126 us (level)
  waiting for transfers between devices: 26.7 us -> 24.3 us
    all_to_all x1, waiting for transfers between devices: 8 us -> 5.97 us  [step(): line = lax.all_to_all(piece, ('grp', 'dp'), 0, 0, tiled=True)]
    pallas_call x1 -> x2, Pallas kernels: 2.9 us -> 3.57 us  [the longest x1 2.02 us: edges(): pl.pallas_call(edges_kernel, out_shape=[out, out], in_specs=[pl.BlockSpec...]
  transfers between devices with their start and end apart: 15 -> 15, of which waited for: 7 -> 7; matrix products, arithmetic and copies ran while one was open for 0% -> 0% of each run, Pallas kernels for 11% -> 13%
where the time goes in v3:
time: 126 us; the launch traced here: 125 us
  Pallas kernels  41.3 us (33%)
  starting transfers between devices  32.7 us (26%)
  waiting for transfers between devices  24.3 us (19%)
  blocking collectives  22.4 us (18%)
  local copies, waits for them, and re-layouts  2.42 us (2%)
  other arithmetic  1.31 us (1%)
    pallas_call x1, Pallas kernels, pointwise(): pl.pallas_call(functools.partial(pointwise_kernel, nx=nx, taps=taps, inv_...  22.4 us
    pallas_call x2, Pallas kernels, conv(): pl.pallas_call(functools.partial(conv_kernel, taps=taps), out_shape=jax.S...  13.7 us
    all_to_all x1, blocking collectives, spread(): return lax.all_to_all(copies, axis, 0, 0, tiled=True)  12.3 us
    all_to_all x1, starting transfers between devices, step(): line = lax.all_to_all(piece, ('grp', 'dp'), 0, 0, tiled=True)  12.2 us
    all_to_all x1, blocking collectives, step(): lax.all_to_all(jnp.concatenate([line_sum, rest], axis=1), 'dp', 0, 0, til...  10.1 us
    ppermute x1, starting transfers between devices, step(): bot = lax.ppermute(head, 'row', [(i + 1, i) for i in range(row - 1)])  6.48 us
    all_to_all x1, waiting for transfers between devices, step(): line = lax.all_to_all(piece, ('grp', 'dp'), 0, 0, tiled=True)  5.97 us
    ppermute x1, waiting for transfers between devices, step(): bot = lax.ppermute(head, 'row', [(i + 1, i) for i in range(row - 1)])  5.51 us
  transfers between devices with their start and end apart: 15, of which 7 were waited for; matrix products, arithmetic and copies ran while one was open for 0% of the time, Pallas kernels for 13%

profile of v3, /device:TPU:1, one launch (start us, length us, event | category | flops | bytes accessed | tf_op | source)
XLA Modules:
  0.0 125.2 jit_solution(8828782699480153334)
XLA Ops:
  0.6 1.6 %prep.1 = (bf16[32,16,256]{2,1,0:T(8,128)(2,1)}, bf16[64,256]{1,0:T(8,128)(2,1)}) custom-call(bf16[1,16,1024]{2,1,0:T(8,128)(2,1)} %w_in.1, bf16[1,64,256]{2,1,0:T(8,128)(2,1)} %w_out.1, bf16[1,7,7,256]{3,2,1,0:T(8,128)(2,1)} %kernel.1, bf16[1,256]{1,0:T(2,128)(2,1)} %gain.1, bf16[1,256]{1,0:T(2,128)(2,1)} %scale.1), custom_call_target="tpu_custom_call" | custom-call | tf_op jit(solution)/shard_map/prep/pallas_call | solution.py:65
  2.2 12.2 %all-to-all-start = ((bf16[32,16,256]{2,1,0:T(8,128)(2,1)}), bf16[32,16,256]{2,1,0:T(8,128)(2,1)S(1)}, u32[]{:S(2)}, u32[]{:S(2)}) async-start(bf16[32,16,256]{2,1,0:T(8,128)(2,1)} %get-tuple-element.18), calls=%async_computation | async-start | bytes 524288 | tf_op jit(solution)/shard_map/all_to_all | solution.py:414
  14.3 2.0 %edges.1 = (bf16[3,256,256]{2,1,0:T(8,128)(2,1)}, bf16[3,256,256]{2,1,0:T(8,128)(2,1)}) custom-call(bf16[1,1,8,256,256]{4,3,2,1,0:T(8,128)(2,1)} %images.1), custom_call_target="tpu_custom_call" | custom-call | tf_op jit(solution)/shard_map/edges/pallas_call | solution.py:37
  16.4 4.0 %collective-permute-start.7 = (bf16[3,256,256]{2,1,0:T(8,128)(2,1)}, bf16[3,256,256]{2,1,0:T(8,128)(2,1)S(1)}, u32[]{:S(2)}, u32[]{:S(2)}) collective-permute-start(bf16[3,256,256]{2,1,0:T(8,128)(2,1)} %get-tuple-element.19), channel_id=1, source_target_pairs={{0,1},{1,2},{2,3},{3,4},{4,5},{5,6},{6,7},{8,9},{9,10},{10,11},{11... | collective-permute-start | bytes 1179656 | tf_op jit(solution)/shard_map/ppermute | solution.py:411
  20.3 6.0 %all-to-all-done.refs_0_ = bf16[32,16,256]{2,1,0:T(8,128)(2,1)S(1)} async-done(((bf16[32,16,256]{2,1,0:T(8,128)(2,1)}), bf16[32,16,256]{2,1,0:T(8,128)(2,1)S(1)}, u32[]{:S(2)}, u32[]{:S(2)}) %all-to-all-start) | async-done | bytes 262176 | tf_op jit(solution)/shard_map/all_to_all | solution.py:414
  26.3 2.5 %collective-permute-start.5 = (bf16[32,16,256]{2,1,0:T(8,128)(2,1)S(1)}, bf16[32,16,256]{2,1,0:T(8,128)(2,1)S(1)}, u32[]{:S(2)}, u32[]{:S(2)}) collective-permute-start(bf16[32,16,256]{2,1,0:T(8,128)(2,1)S(1)} %all-to-all-done.refs_0_), channel_id=1, source_target_pairs={{0,6},{1,7},{2,0},{3,1},{4,2},{5,3},{6,4},{7,5},{8,14},{9,15},{10,... | collective-permute-start | bytes 786440 | tf_op jit(solution)/shard_map/ppermute | solution.py:415
  28.8 0.5 collective-permute-start.3
  29.3 0.6 collective-permute-start.1
  29.9 0.0 copy-done.3
  29.9 1.5 %collective-permute-start.9 = (bf16[64,256]{1,0:T(8,128)(2,1)S(1)}, bf16[64,256]{1,0:T(8,128)(2,1)S(1)}, u32[]{:S(2)}, u32[]{:S(2)}) collective-permute-start(bf16[64,256]{1,0:T(8,128)(2,1)S(1)} %copy-done.3), channel_id=1, source_target_pairs={{0,128},{128,0},{1,129},{129,1},{2,130},{130,2},{3,131},{131,3},{4... | collective-permute-start | bytes 98312 | tf_op jit(solution)/shard_map/ppermute | solution.py:413
  31.4 5.2 %collective-permute-done.9.men.refs_14_ = bf16[64,256]{1,0:T(8,128)(2,1)S(1)} collective-permute-done((bf16[64,256]{1,0:T(8,128)(2,1)S(1)}, bf16[64,256]{1,0:T(8,128)(2,1)S(1)}, u32[]{:S(2)}, u32[]{:S(2)}) %collective-permute-start.9) | collective-permute-done | bytes 32800 | tf_op jit(solution)/shard_map/ppermute | solution.py:413
  36.6 6.5 %collective-permute-start.8 = (bf16[3,256,256]{2,1,0:T(8,128)(2,1)}, bf16[3,256,256]{2,1,0:T(8,128)(2,1)S(1)}, u32[]{:S(2)}, u32[]{:S(2)}) collective-permute-start(bf16[3,256,256]{2,1,0:T(8,128)(2,1)} %get-tuple-element.20), channel_id=1, source_target_pairs={{1,0},{2,1},{3,2},{4,3},{5,4},{6,5},{7,6},{9,8},{10,9},{11,10},{12... | collective-permute-start | bytes 1179656 | tf_op jit(solution)/shard_map/ppermute | solution.py:412
  43.1 0.0 collective-permute-done.7.top.refs_11_
  43.1 0.1 collective-permute-start
  43.2 0.0 collective-permute-done.5.refs_6_
  43.2 0.0 copy-start.5
  43.2 0.5 collective-permute-start.6
  43.7 0.0 collective-permute-done.3.refs_4_
  43.7 0.1 collective-permute-start.4
  43.8 0.0 collective-permute-done.1.refs_2_
  43.8 0.8 collective-permute-start.2
  44.6 5.5 %collective-permute-done.8.bot.refs_12_ = bf16[3,256,256]{2,1,0:T(8,128)(2,1)S(1)} collective-permute-done((bf16[3,256,256]{2,1,0:T(8,128)(2,1)}, bf16[3,256,256]{2,1,0:T(8,128)(2,1)S(1)}, u32[]{:S(2)}, u32[]{:S(2)}) %collective-permute-start.8) | collective-permute-done | bytes 393248 | tf_op jit(solution)/shard_map/ppermute | solution.py:412
  50.2 0.8 copy-done.1
  50.9 6.9 %shard_map.110.refs_9_ = f32[2,8,256,128]{3,2,1,0:T(8,128)} custom-call(bf16[8,256,256]{2,1,0:T(8,128)(2,1)} %bitcast.15, bf16[3,256,256]{2,1,0:T(8,128)(2,1)} %copy-done, bf16[3,256,256]{2,1,0:T(8,128)(2,1)} %copy-done.1, bf16[64,256]{1,0:T(8,128)(2,1)} %get-tuple-element.21.own.refs_13_, bf16[64,256]{1,0:T(8,128)(2,1)} %copy-done.4), custom_call_target="tpu_custom_call" | custom-call | tf_op jit(solution)/shard_map/pallas_call | solution.py:170
  57.8 6.8 %shard_map.109.refs_8_ = f32[2,8,256,128]{3,2,1,0:T(8,128)} custom-call(bf16[8,256,256]{2,1,0:T(8,128)(2,1)} %bitcast.16, bf16[3,256,256]{2,1,0:T(8,128)(2,1)} %copy-done, bf16[3,256,256]{2,1,0:T(8,128)(2,1)} %copy-done.1, bf16[64,256]{1,0:T(8,128)(2,1)} %get-tuple-element.21.own.refs_13_, bf16[64,256]{1,0:T(8,128)(2,1)} %copy-done.4), custom_call_target="tpu_custom_call" | custom-call | tf_op jit(solution)/shard_map/pallas_call | solution.py:170
  64.6 0.0 copy-done.5
  64.7 0.0 collective-permute-done.refs_1_
  64.7 0.0 collective-permute-done.6.refs_7_
  64.7 0.0 collective-permute-done.4.refs_5_
  64.7 0.0 collective-permute-done.2.refs_3_
  64.7 0.7 copy-done.8
  65.4 0.1 copy-done.9
  65.5 0.1 copy-done.10
  65.6 0.7 copy-done.11
  66.3 22.4 %pointwise.1 = (bf16[2048,256]{1,0:T(8,128)(2,1)}, bf16[4,264,256]{2,1,0:T(8,128)(2,1)}, bf16[4,264,256]{2,1,0:T(8,128)(2,1)}) custom-call(bf16[32,16,256]{2,1,0:T(8,128)(2,1)} %copy-done.2, bf16[32,16,256]{2,1,0:T(8,128)(2,1)} %copy-done.8, bf16[32,16,256]{2,1,0:T(8,128)(2,1)} %copy-done.7, bf16[32,16,256]{2,1,0:T(8,128)(2,1)} %copy-done.11, ...), custom_call_target="tpu_custom_call" | custom-call | tf_op jit(solution)/shard_map/pointwise/pallas_call | solution.py:359
  88.7 0.3 collective-permute-start.10
  89.0 2.1 %collective-permute-done.10 = bf16[4,264,256]{2,1,0:T(8,128)(2,1)S(1)} collective-permute-done((bf16[4,264,256]{2,1,0:T(8,128)(2,1)}, bf16[4,264,256]{2,1,0:T(8,128)(2,1)S(1)}, u32[]{:S(2)}, u32[]{:S(2)}) %collective-permute-start.10) | collective-permute-done | bytes 540704 | tf_op jit(solution)/shard_map/ppermute | solution.py:426
  91.2 1.2 add_convert_fusion
  92.4 0.1 collective-permute-start.11
  92.5 2.7 %collective-permute-start.13 = (bf16[264,256]{1,0:T(8,128)(2,1)S(1)}, bf16[264,256]{1,0:T(8,128)(2,1)S(1)}, u32[]{:S(2)}, u32[]{:S(2)}) collective-permute-start(bf16[264,256]{1,0:T(8,128)(2,1)S(1)} %get-tuple-element.31), channel_id=1, source_target_pairs={{0,6},{1,7},{2,0},{3,1},{4,2},{5,3},{6,4},{7,5},{8,14},{9,15},{10,... | collective-permute-start | bytes 405512 | tf_op jit(solution)/shard_map/ppermute | solution.py:428
  95.1 0.5 collective-permute-start.12
  95.7 3.0 %collective-permute-done.11 = bf16[264,256]{1,0:T(8,128)(2,1)S(1)} collective-permute-done((bf16[264,256]{1,0:T(8,128)(2,1)S(1)}, bf16[264,256]{1,0:T(8,128)(2,1)S(1)}, u32[]{:S(2)}, u32[]{:S(2)}) %collective-permute-start.11) | collective-permute-done | bytes 135200 | tf_op jit(solution)/shard_map/ppermute | solution.py:428
  98.7 1.8 %collective-permute-done.13 = bf16[264,256]{1,0:T(8,128)(2,1)S(1)} collective-permute-done((bf16[264,256]{1,0:T(8,128)(2,1)S(1)}, bf16[264,256]{1,0:T(8,128)(2,1)S(1)}, u32[]{:S(2)}, u32[]{:S(2)}) %collective-permute-start.13) | collective-permute-done | bytes 135200 | tf_op jit(solution)/shard_map/ppermute | solution.py:428
  100.5 0.6 collective-permute-done.12
  101.1 0.1 fusion.2
  101.2 10.1 %all_to_all.15 = bf16[16,24,256]{2,1,0:T(8,128)(2,1)S(1)} all-to-all(bf16[16,24,256]{2,1,0:T(8,128)(2,1)S(1)} %pad_maximum_fusion), channel_id=1, replica_groups=mesh['grp'=2,'dp'=16,'row'=8] {'dp'}, dimensions={0} | all-to-all | bytes 393216 | tf_op jit(solution)/shard_map/all_to_all | solution.py:436
  111.4 12.3 %all_to_all.16.done = bf16[8,24,256]{2,1,0:T(8,128)(2,1)} all-to-all(bf16[8,24,256]{2,1,0:T(8,128)(2,1)S(1)} %broadcast_in_dim.5), channel_id=1, replica_groups=mesh['grp'=2,'dp'=16,'row'=8] {'row'}, dimensions={0} | all-to-all | bytes 196608 | tf_op jit(solution)/shard_map/all_to_all | solution.py:395
  123.7 1.6 %finish.1 = (f32[1,16,1024]{2,1,0:T(8,128)}, f32[1,64,256]{2,1,0:T(8,128)}, f32[7,7,1,256]{3,2,1,0:T(1,128)}, f32[1,256]{1,0:T(1,128)}, f32[1,256]{1,0:T(1,128)}) custom-call(bf16[8,24,256]{2,1,0:T(8,128)(2,1)} %all_to_all.16.done), custom_call_target="tpu_custom_call" | custom-call | tf_op jit(solution)/shard_map/finish/pallas_call | solution.py:92
  (23 shorter events, 0.1 us)
Async XLA Ops:
  2.2 27.7 %copy-start.3 = (bf16[64,256]{1,0:T(8,128)(2,1)S(1)}, bf16[64,256]{1,0:T(8,128)(2,1)}, u32[]{:S(2)}) copy-start(bf16[64,256]{1,0:T(8,128)(2,1)} %get-tuple-element.21.own.refs_13_) | copy-start | bytes 98308
  2.2 24.1 %all-to-all-start = ((bf16[32,16,256]{2,1,0:T(8,128)(2,1)}), bf16[32,16,256]{2,1,0:T(8,128)(2,1)S(1)}, u32[]{:S(2)}, u32[]{:S(2)}) async-start(bf16[32,16,256]{2,1,0:T(8,128)(2,1)} %get-tuple-element.18), calls=%async_computation | async-start | bytes 524288 | tf_op jit(solution)/shard_map/all_to_all | solution.py:414
  16.4 26.7 %collective-permute-start.7 = (bf16[3,256,256]{2,1,0:T(8,128)(2,1)}, bf16[3,256,256]{2,1,0:T(8,128)(2,1)S(1)}, u32[]{:S(2)}, u32[]{:S(2)}) collective-permute-start(bf16[3,256,256]{2,1,0:T(8,128)(2,1)} %get-tuple-element.19), channel_id=1, source_target_pairs={{0,1},{1,2},{2,3},{3,4},{4,5},{5,6},{6,7},{8,9},{9,10},{10,11},{11... | collective-permute-start | bytes 1179656 | tf_op jit(solution)/shard_map/ppermute | solution.py:411
  26.3 38.3 %copy-start.2 = (bf16[32,16,256]{2,1,0:T(8,128)(2,1)}, bf16[32,16,256]{2,1,0:T(8,128)(2,1)S(1)}, u32[]{:S(2)}) copy-start(bf16[32,16,256]{2,1,0:T(8,128)(2,1)S(1)} %all-to-all-done.refs_0_) | copy-start | bytes 786436
  26.3 16.9 %collective-permute-start.5 = (bf16[32,16,256]{2,1,0:T(8,128)(2,1)S(1)}, bf16[32,16,256]{2,1,0:T(8,128)(2,1)S(1)}, u32[]{:S(2)}, u32[]{:S(2)}) collective-permute-start(bf16[32,16,256]{2,1,0:T(8,128)(2,1)S(1)} %all-to-all-done.refs_0_), channel_id=1, source_target_pairs={{0,6},{1,7},{2,0},{3,1},{4,2},{5,3},{6,4},{7,5},{8,14},{9,15},{10,... | collective-permute-start | bytes 786440 | tf_op jit(solution)/shard_map/ppermute | solution.py:415
  28.8 14.9 %collective-permute-start.3 = (bf16[32,16,256]{2,1,0:T(8,128)(2,1)S(1)}, bf16[32,16,256]{2,1,0:T(8,128)(2,1)S(1)}, u32[]{:S(2)}, u32[]{:S(2)}) collective-permute-start(bf16[32,16,256]{2,1,0:T(8,128)(2,1)S(1)} %all-to-all-done.refs_0_), channel_id=1, source_target_pairs={{0,4},{1,5},{2,6},{3,7},{4,0},{5,1},{6,2},{7,3},{8,12},{9,13},{10,... | collective-permute-start | bytes 786440 | tf_op jit(solution)/shard_map/ppermute | solution.py:415
  29.3 14.5 %collective-permute-start.1 = (bf16[32,16,256]{2,1,0:T(8,128)(2,1)S(1)}, bf16[32,16,256]{2,1,0:T(8,128)(2,1)S(1)}, u32[]{:S(2)}, u32[]{:S(2)}) collective-permute-start(bf16[32,16,256]{2,1,0:T(8,128)(2,1)S(1)} %all-to-all-done.refs_0_), channel_id=1, source_target_pairs={{0,2},{1,3},{2,4},{3,5},{4,6},{5,7},{6,0},{7,1},{8,10},{9,11},{10,... | collective-permute-start | bytes 786440 | tf_op jit(solution)/shard_map/ppermute | solution.py:415
  29.9 6.7 %collective-permute-start.9 = (bf16[64,256]{1,0:T(8,128)(2,1)S(1)}, bf16[64,256]{1,0:T(8,128)(2,1)S(1)}, u32[]{:S(2)}, u32[]{:S(2)}) collective-permute-start(bf16[64,256]{1,0:T(8,128)(2,1)S(1)} %copy-done.3), channel_id=1, source_target_pairs={{0,128},{128,0},{1,129},{129,1},{2,130},{130,2},{3,131},{131,3},{4... | collective-permute-start | bytes 98312 | tf_op jit(solution)/shard_map/ppermute | solution.py:413
  36.6 13.6 %copy-start.4 = (bf16[64,256]{1,0:T(8,128)(2,1)}, bf16[64,256]{1,0:T(8,128)(2,1)S(1)}, u32[]{:S(2)}) copy-start(bf16[64,256]{1,0:T(8,128)(2,1)S(1)} %collective-permute-done.9.men.refs_14_) | copy-start | bytes 98308
  36.6 13.6 %collective-permute-start.8 = (bf16[3,256,256]{2,1,0:T(8,128)(2,1)}, bf16[3,256,256]{2,1,0:T(8,128)(2,1)S(1)}, u32[]{:S(2)}, u32[]{:S(2)}) collective-permute-start(bf16[3,256,256]{2,1,0:T(8,128)(2,1)} %get-tuple-element.20), channel_id=1, source_target_pairs={{1,0},{2,1},{3,2},{4,3},{5,4},{6,5},{7,6},{9,8},{10,9},{11,10},{12... | collective-permute-start | bytes 1179656 | tf_op jit(solution)/shard_map/ppermute | solution.py:412
  43.1 7.1 %copy-start = (bf16[3,256,256]{2,1,0:T(8,128)(2,1)}, bf16[3,256,256]{2,1,0:T(8,128)(2,1)S(1)}, u32[]{:S(2)}) copy-start(bf16[3,256,256]{2,1,0:T(8,128)(2,1)S(1)} %collective-permute-done.7.top.refs_11_) | copy-start | bytes 1179652
  43.1 21.5 %collective-permute-start = (bf16[32,16,256]{2,1,0:T(8,128)(2,1)S(1)}, bf16[32,16,256]{2,1,0:T(8,128)(2,1)S(1)}, u32[]{:S(2)}, u32[]{:S(2)}) collective-permute-start(bf16[32,16,256]{2,1,0:T(8,128)(2,1)S(1)} %all-to-all-done.refs_0_), channel_id=1, source_target_pairs={{0,1},{1,0},{2,3},{3,2},{4,5},{5,4},{6,7},{7,6},{8,9},{9,8},{10,11... | collective-permute-start | bytes 786440 | tf_op jit(solution)/shard_map/ppermute | solution.py:418
  43.2 21.4 %copy-start.5 = (bf16[32,16,256]{2,1,0:T(8,128)(2,1)}, bf16[32,16,256]{2,1,0:T(8,128)(2,1)S(1)}, u32[]{:S(2)}) copy-start(bf16[32,16,256]{2,1,0:T(8,128)(2,1)S(1)} %collective-permute-done.5.refs_6_) | copy-start | bytes 786436
  43.2 21.4 %collective-permute-start.6 = (bf16[32,16,256]{2,1,0:T(8,128)(2,1)S(1)}, bf16[32,16,256]{2,1,0:T(8,128)(2,1)S(1)}, u32[]{:S(2)}, u32[]{:S(2)}) collective-permute-start(bf16[32,16,256]{2,1,0:T(8,128)(2,1)S(1)} %collective-permute-done.5.refs_6_), channel_id=1, source_target_pairs={{0,1},{1,0},{2,3},{3,2},{4,5},{5,4},{6,7},{7,6},{8,9},{9,8},{10,11... | collective-permute-start | bytes 786440 | tf_op jit(solution)/shard_map/ppermute | solution.py:418
  43.7 20.9 %copy-start.6 = (bf16[32,16,256]{2,1,0:T(8,128)(2,1)}, bf16[32,16,256]{2,1,0:T(8,128)(2,1)S(1)}, u32[]{:S(2)}) copy-start(bf16[32,16,256]{2,1,0:T(8,128)(2,1)S(1)} %collective-permute-done.3.refs_4_) | copy-start | bytes 786436
  43.7 21.0 %collective-permute-start.4 = (bf16[32,16,256]{2,1,0:T(8,128)(2,1)S(1)}, bf16[32,16,256]{2,1,0:T(8,128)(2,1)S(1)}, u32[]{:S(2)}, u32[]{:S(2)}) collective-permute-start(bf16[32,16,256]{2,1,0:T(8,128)(2,1)S(1)} %collective-permute-done.3.refs_4_), channel_id=1, source_target_pairs={{0,1},{1,0},{2,3},{3,2},{4,5},{5,4},{6,7},{7,6},{8,9},{9,8},{10,11... | collective-permute-start | bytes 786440 | tf_op jit(solution)/shard_map/ppermute | solution.py:418
  43.8 20.8 %copy-start.7 = (bf16[32,16,256]{2,1,0:T(8,128)(2,1)}, bf16[32,16,256]{2,1,0:T(8,128)(2,1)S(1)}, u32[]{:S(2)}) copy-start(bf16[32,16,256]{2,1,0:T(8,128)(2,1)S(1)} %collective-permute-done.1.refs_2_) | copy-start | bytes 786436
  43.8 20.9 %collective-permute-start.2 = (bf16[32,16,256]{2,1,0:T(8,128)(2,1)S(1)}, bf16[32,16,256]{2,1,0:T(8,128)(2,1)S(1)}, u32[]{:S(2)}, u32[]{:S(2)}) collective-permute-start(bf16[32,16,256]{2,1,0:T(8,128)(2,1)S(1)} %collective-permute-done.1.refs_2_), channel_id=1, source_target_pairs={{0,1},{1,0},{2,3},{3,2},{4,5},{5,4},{6,7},{7,6},{8,9},{9,8},{10,11... | collective-permute-start | bytes 786440 | tf_op jit(solution)/shard_map/ppermute | solution.py:418
  50.2 0.8 copy-start.1
  64.7 0.7 copy-start.8
  64.7 0.8 copy-start.9
  64.7 0.9 copy-start.10
  65.6 0.7 copy-start.11
  88.7 2.4 %collective-permute-start.10 = (bf16[4,264,256]{2,1,0:T(8,128)(2,1)}, bf16[4,264,256]{2,1,0:T(8,128)(2,1)S(1)}, u32[]{:S(2)}, u32[]{:S(2)}) collective-permute-start(bf16[4,264,256]{2,1,0:T(8,128)(2,1)} %get-tuple-element.24), channel_id=1, source_target_pairs={{0,1},{1,0},{2,3},{3,2},{4,5},{5,4},{6,7},{7,6},{8,9},{9,8},{10,11... | collective-permute-start | bytes 1622024 | tf_op jit(solution)/shard_map/ppermute | solution.py:426
  92.4 6.3 %collective-permute-start.11 = (bf16[264,256]{1,0:T(8,128)(2,1)S(1)}, bf16[264,256]{1,0:T(8,128)(2,1)S(1)}, u32[]{:S(2)}, u32[]{:S(2)}) collective-permute-start(bf16[264,256]{1,0:T(8,128)(2,1)S(1)} %get-tuple-element.30), channel_id=1, source_target_pairs={{0,2},{1,3},{2,4},{3,5},{4,6},{5,7},{6,0},{7,1},{8,10},{9,11},{10,... | collective-permute-start | bytes 405512 | tf_op jit(solution)/shard_map/ppermute | solution.py:428
  92.5 8.0 %collective-permute-start.13 = (bf16[264,256]{1,0:T(8,128)(2,1)S(1)}, bf16[264,256]{1,0:T(8,128)(2,1)S(1)}, u32[]{:S(2)}, u32[]{:S(2)}) collective-permute-start(bf16[264,256]{1,0:T(8,128)(2,1)S(1)} %get-tuple-element.31), channel_id=1, source_target_pairs={{0,6},{1,7},{2,0},{3,1},{4,2},{5,3},{6,4},{7,5},{8,14},{9,15},{10,... | collective-permute-start | bytes 405512 | tf_op jit(solution)/shard_map/ppermute | solution.py:428
  95.1 6.0 %collective-permute-start.12 = (bf16[264,256]{1,0:T(8,128)(2,1)S(1)}, bf16[264,256]{1,0:T(8,128)(2,1)S(1)}, u32[]{:S(2)}, u32[]{:S(2)}) collective-permute-start(bf16[264,256]{1,0:T(8,128)(2,1)S(1)} %get-tuple-element.32), channel_id=1, source_target_pairs={{0,4},{1,5},{2,6},{3,7},{4,0},{5,1},{6,2},{7,3},{8,12},{9,13},{10,... | collective-permute-start | bytes 405512 | tf_op jit(solution)/shard_map/ppermute | solution.py:428

commit v4 on v2

--- a/solution.py
+++ b/solution.py
@@ -12,8 +12,8 @@
 INV_SQRT_TAU = 0.3989422804014327
 BF = jnp.bfloat16
 F32 = jnp.float32
-SUB = 512
-TILE = 512
+SUB = 1024
+TILE = 1024
 LEFT = 8
 
 
@@ -99,6 +99,8 @@
 def fill_padded(pad, img, top, bot, edge):
     rows, cols, chans = img.shape
     zero = jnp.zeros((8, 128), F32)
+    me = lax.axis_index("row")
+    first, last = me == 0, me == lax.axis_size("row") - 1
     for cb in range(chans // 128):
         lanes = slice(cb * 128, cb * 128 + 128)
         for r in range(rows + 2 * edge):
@@ -110,7 +112,10 @@
                 ref, q = bot, r - rows - edge
             pad[cb, r, 0:LEFT, :] = zero
             pad[cb, r, LEFT + cols : LEFT + cols + 8, :] = zero
-            pad[cb, r, LEFT : LEFT + cols, :] = ref[q, :, lanes].astype(F32)
+            line = ref[q, :, lanes].astype(F32)
+            if r < edge or r >= rows + edge:
+                line = jnp.where(first if r < edge else last, 0.0, line)
+            pad[cb, r, LEFT : LEFT + cols, :] = line
 
 
 def tree(terms):
@@ -139,15 +144,19 @@
         at = pl.multiple_of(wb * 16, 16)
         w0 = pl.multiple_of(base + at, 16)
         accs = {}
-        for j in range(taps):
-            vs = [
-                pad[0, r, pl.ds(w0 + (LEFT - edge + j), 16), :].astype(BF) for r in range(rows + 2 * edge)
-            ]
+        for j0 in range(0, taps, 2):
+            pair = range(j0, min(j0 + 2, taps))
+            vs = {
+                (j, r): pad[0, r, pl.ds(w0 + (LEFT - edge + j), 16), :].astype(BF)
+                for j in pair
+                for r in range(rows + 2 * edge)
+            }
             for s in range(2):
-                w = [wide_taps[s, i * taps + j] for i in range(taps)]
+                w = {(j, i): wide_taps[s, i * taps + j] for j in pair for i in range(taps)}
                 for h in range(rows):
-                    term = tree([vs[h + i] * w[i] for i in range(taps)]).astype(F32)
-                    accs[s, h] = term if j == 0 else accs[s, h] + term
+                    term = tree([tree([vs[j, h + i] * w[j, i] for i in range(taps)]) for j in pair])
+                    term = term.astype(F32)
+                    accs[s, h] = term if j0 == 0 else accs[s, h] + term
         for h in range(rows):
             for s in range(2):
                 filt[s, h, pl.ds(at, 16), :] = accs[s, h]
@@ -400,8 +409,8 @@
     chips = lambda k: [(i, (i + 2 * k) % row) for i in range(row)]
 
     head, tail, piece, small = prep(images, w_in, w_out, kernel, gain, scale, grp * dp)
-    top = lax.ppermute(tail, "row", [(i, i + 1) for i in range(row - 1)])
-    bot = lax.ppermute(head, "row", [(i + 1, i) for i in range(row - 1)])
+    top = lax.ppermute(tail, "row", ring("row", 1))
+    bot = lax.ppermute(head, "row", ring("row", -1))
     men_small = lax.ppermute(small, "grp", ring("grp", 1))
     line = lax.all_to_all(piece, ("grp", "dp"), 0, 0, tiled=True)
     hops = [line] + [lax.ppermute(line, "row", chips(k)) for k in range(1, nx)]

time: 127 us -> 124 us (0.976)
  starting transfers between devices: 32.4 us -> 28.9 us
  waiting for transfers between devices: 26.7 us -> 28.2 us
    ppermute x2, starting transfers between devices: 10.4 us -> 6.64 us  [the longest x1 4.58 us: step(): bot = lax.ppermute(head, 'row', ring('row', -1))]
    all_to_all x1, waiting for transfers between devices: 8 us -> 9.9 us  [step(): line = lax.all_to_all(piece, ('grp', 'dp'), 0, 0, tiled=True)]
    ppermute x2, waiting for transfers between devices: 5.72 us -> 3.83 us  [the longest x1 3.83 us: step(): bot = lax.ppermute(head, 'row', ring('row', -1))]
    ppermute x3, waiting for transfers between devices: 0.01 us -> 1.45 us  [step(): hops = [line] + [lax.ppermute(line, 'row', chips(k)) for k in range(1, nx)]]
  transfers between devices with their start and end apart: 15 -> 15, of which waited for: 7 -> 8; matrix products, arithmetic and copies ran while one was open for 0% -> 0% of each run, Pallas kernels for 11% -> 11%
where the time goes in v4:
time: 124 us
  Pallas kernels  39.7 us (32%)
  starting transfers between devices  28.9 us (23%)
  waiting for transfers between devices  28.2 us (23%)
  blocking collectives  22.4 us (18%)
  local copies, waits for them, and re-layouts  2.41 us (2%)
  other arithmetic  1.31 us (1%)
    pallas_call x1, Pallas kernels, pointwise(): pl.pallas_call(functools.partial(pointwise_kernel, nx=nx, taps=taps, inv_...  22 us
    pallas_call x2, Pallas kernels, conv(): pl.pallas_call(functools.partial(conv_kernel, taps=taps), out_shape=jax.S...  13.3 us
    all_to_all x1, blocking collectives, spread(): return lax.all_to_all(copies, axis, 0, 0, tiled=True)  12.3 us
    all_to_all x1, starting transfers between devices, step(): line = lax.all_to_all(piece, ('grp', 'dp'), 0, 0, tiled=True)  12 us
    all_to_all x1, blocking collectives, step(): lax.all_to_all(jnp.concatenate([line_sum, rest], axis=1), 'dp', 0, 0, til...  10.1 us
    all_to_all x1, waiting for transfers between devices, step(): line = lax.all_to_all(piece, ('grp', 'dp'), 0, 0, tiled=True)  9.9 us
    ppermute x3, waiting for transfers between devices, step(): sent = [lax.ppermute(chip[k], 'row', chips(k)) for k in range(1, nx)]  5.43 us
    ppermute x1, waiting for transfers between devices, step(): men_small = lax.ppermute(small, 'grp', ring('grp', 1))  5.42 us
  transfers between devices with their start and end apart: 15, of which 8 were waited for; matrix products, arithmetic and copies ran while one was open for 0% of the time, Pallas kernels for 11%

profile of v4, /device:TPU:1, one launch (start us, length us, event | category | flops | bytes accessed | tf_op | source)
XLA Modules:
  0.0 123.7 jit_solution(471234806366063876)
XLA Ops:
  0.6 2.9 %prep.1 = (bf16[3,256,256]{2,1,0:T(8,128)(2,1)}, bf16[3,256,256]{2,1,0:T(8,128)(2,1)}, bf16[32,16,256]{2,1,0:T(8,128)(2,1)}, bf16[64,256]{1,0:T(8,128)(2,1)}) custom-call(bf16[1,1,8,256,256]{4,3,2,1,0:T(8,128)(2,1)} %images.1, bf16[1,16,1024]{2,1,0:T(8,128)(2,1)} %w_in.1, bf16[1,64,256]{2,1,0:T(8,128)(2,1)} %w_out.1, bf16[1,7,7,256]{3,2,1,0:T(8,128)(2,1)} %kernel.1, ...), custom_call_target="tpu_custom_call" | custom-call | tf_op jit(solution)/shard_map/prep/pallas_call | solution.py:54
  3.5 12.0 %all-to-all-start = ((bf16[32,16,256]{2,1,0:T(8,128)(2,1)}), bf16[32,16,256]{2,1,0:T(8,128)(2,1)S(1)}, u32[]{:S(2)}, u32[]{:S(2)}) async-start(bf16[32,16,256]{2,1,0:T(8,128)(2,1)} %get-tuple-element.18), calls=%async_computation | async-start | bytes 524288 | tf_op jit(solution)/shard_map/all_to_all | solution.py:415
  15.6 2.1 %collective-permute-start.7 = (bf16[3,256,256]{2,1,0:T(8,128)(2,1)}, bf16[3,256,256]{2,1,0:T(8,128)(2,1)S(1)}, u32[]{:S(2)}, u32[]{:S(2)}) collective-permute-start(bf16[3,256,256]{2,1,0:T(8,128)(2,1)} %get-tuple-element.19), channel_id=1, source_target_pairs={{0,1},{1,2},{2,3},{3,4},{4,5},{5,6},{6,7},{7,0},{8,9},{9,10},{10,1... | collective-permute-start | bytes 1179656 | tf_op jit(solution)/shard_map/ppermute | solution.py:412
  17.6 9.9 %all-to-all-done.refs_0_ = bf16[32,16,256]{2,1,0:T(8,128)(2,1)S(1)} async-done(((bf16[32,16,256]{2,1,0:T(8,128)(2,1)}), bf16[32,16,256]{2,1,0:T(8,128)(2,1)S(1)}, u32[]{:S(2)}, u32[]{:S(2)}) %all-to-all-start) | async-done | bytes 262176 | tf_op jit(solution)/shard_map/all_to_all | solution.py:415
  27.5 2.5 %collective-permute-start.5 = (bf16[32,16,256]{2,1,0:T(8,128)(2,1)S(1)}, bf16[32,16,256]{2,1,0:T(8,128)(2,1)S(1)}, u32[]{:S(2)}, u32[]{:S(2)}) collective-permute-start(bf16[32,16,256]{2,1,0:T(8,128)(2,1)S(1)} %all-to-all-done.refs_0_), channel_id=1, source_target_pairs={{0,6},{1,7},{2,0},{3,1},{4,2},{5,3},{6,4},{7,5},{8,14},{9,15},{10,... | collective-permute-start | bytes 786440 | tf_op jit(solution)/shard_map/ppermute | solution.py:416
  30.0 0.5 collective-permute-start.3
  30.5 0.6 collective-permute-start.1
  31.2 1.5 %collective-permute-start.9 = (bf16[64,256]{1,0:T(8,128)(2,1)}, bf16[64,256]{1,0:T(8,128)(2,1)S(1)}, u32[]{:S(2)}, u32[]{:S(2)}) collective-permute-start(bf16[64,256]{1,0:T(8,128)(2,1)} %get-tuple-element.21.own.refs_13_), channel_id=1, source_target_pairs={{0,128},{128,0},{1,129},{129,1},{2,130},{130,2},{3,131},{131,3},{4... | collective-permute-start | bytes 98312 | tf_op jit(solution)/shard_map/ppermute | solution.py:414
  32.6 5.4 %collective-permute-done.9.men.refs_14_ = bf16[64,256]{1,0:T(8,128)(2,1)S(1)} collective-permute-done((bf16[64,256]{1,0:T(8,128)(2,1)}, bf16[64,256]{1,0:T(8,128)(2,1)S(1)}, u32[]{:S(2)}, u32[]{:S(2)}) %collective-permute-start.9) | collective-permute-done | bytes 32800 | tf_op jit(solution)/shard_map/ppermute | solution.py:414
  38.0 4.6 %collective-permute-start.8 = (bf16[3,256,256]{2,1,0:T(8,128)(2,1)}, bf16[3,256,256]{2,1,0:T(8,128)(2,1)S(1)}, u32[]{:S(2)}, u32[]{:S(2)}) collective-permute-start(bf16[3,256,256]{2,1,0:T(8,128)(2,1)} %get-tuple-element.20), channel_id=1, source_target_pairs={{0,7},{1,0},{2,1},{3,2},{4,3},{5,4},{6,5},{7,6},{8,15},{9,8},{10,9... | collective-permute-start | bytes 1179656 | tf_op jit(solution)/shard_map/ppermute | solution.py:413
  42.6 0.0 collective-permute-done.7.top.refs_11_
  42.6 0.1 collective-permute-start
  42.7 0.0 collective-permute-done.5.refs_6_
  42.7 0.4 collective-permute-start.6
  43.1 0.0 collective-permute-done.3.refs_4_
  43.1 0.1 collective-permute-start.4
  43.3 1.4 %collective-permute-done.1.refs_2_ = bf16[32,16,256]{2,1,0:T(8,128)(2,1)S(1)} collective-permute-done((bf16[32,16,256]{2,1,0:T(8,128)(2,1)S(1)}, bf16[32,16,256]{2,1,0:T(8,128)(2,1)S(1)}, u32[]{:S(2)}, u32[]{:S(2)}) %collective-permute-start.1) | collective-permute-done | bytes 262176 | tf_op jit(solution)/shard_map/ppermute | solution.py:416
  44.7 1.2 collective-permute-start.2
  45.9 3.8 %collective-permute-done.8.bot.refs_12_ = bf16[3,256,256]{2,1,0:T(8,128)(2,1)S(1)} collective-permute-done((bf16[3,256,256]{2,1,0:T(8,128)(2,1)}, bf16[3,256,256]{2,1,0:T(8,128)(2,1)S(1)}, u32[]{:S(2)}, u32[]{:S(2)}) %collective-permute-start.8) | collective-permute-done | bytes 393248 | tf_op jit(solution)/shard_map/ppermute | solution.py:413
  49.7 0.0 copy-done.3
  49.7 0.0 copy-done
  49.7 0.8 copy-done.1
  50.5 6.6 %shard_map.110.refs_9_ = f32[2,8,256,128]{3,2,1,0:T(8,128)} custom-call(bf16[8,256,256]{2,1,0:T(8,128)(2,1)} %bitcast.15, bf16[3,256,256]{2,1,0:T(8,128)(2,1)} %copy-done, bf16[3,256,256]{2,1,0:T(8,128)(2,1)} %copy-done.1, bf16[64,256]{1,0:T(8,128)(2,1)} %get-tuple-element.21.own.refs_13_, bf16[64,256]{1,0:T(8,128)(2,1)} %copy-done.3), custom_call_target="tpu_custom_call" | custom-call | tf_op jit(solution)/shard_map/pallas_call | solution.py:172
  57.1 6.7 %shard_map.109.refs_8_ = f32[2,8,256,128]{3,2,1,0:T(8,128)} custom-call(bf16[8,256,256]{2,1,0:T(8,128)(2,1)} %bitcast.16, bf16[3,256,256]{2,1,0:T(8,128)(2,1)} %copy-done, bf16[3,256,256]{2,1,0:T(8,128)(2,1)} %copy-done.1, bf16[64,256]{1,0:T(8,128)(2,1)} %get-tuple-element.21.own.refs_13_, bf16[64,256]{1,0:T(8,128)(2,1)} %copy-done.3), custom_call_target="tpu_custom_call" | custom-call | tf_op jit(solution)/shard_map/pallas_call | solution.py:172
  63.7 0.0 copy-done.2
  63.7 0.0 collective-permute-done.refs_1_
  63.8 0.0 collective-permute-done.6.refs_7_
  63.8 0.0 copy-start.8
  63.8 0.0 collective-permute-done.4.refs_5_
  63.8 0.0 collective-permute-done.2.refs_3_
  63.8 0.6 copy-done.7
  64.5 0.1 copy-done.8
  64.6 0.1 copy-done.9
  64.7 0.7 copy-done.10
  65.4 22.0 %pointwise.1 = (bf16[2048,256]{1,0:T(8,128)(2,1)}, bf16[4,264,256]{2,1,0:T(8,128)(2,1)}, bf16[4,264,256]{2,1,0:T(8,128)(2,1)}) custom-call(bf16[32,16,256]{2,1,0:T(8,128)(2,1)} %copy-done.2, bf16[32,16,256]{2,1,0:T(8,128)(2,1)} %copy-done.7, bf16[32,16,256]{2,1,0:T(8,128)(2,1)} %copy-done.6, bf16[32,16,256]{2,1,0:T(8,128)(2,1)} %copy-done.10, ...), custom_call_target="tpu_custom_call" | custom-call | tf_op jit(solution)/shard_map/pointwise/pallas_call | solution.py:361
  87.4 0.1 collective-permute-start.10
  87.5 2.1 %collective-permute-done.10 = bf16[4,264,256]{2,1,0:T(8,128)(2,1)S(1)} collective-permute-done((bf16[4,264,256]{2,1,0:T(8,128)(2,1)}, bf16[4,264,256]{2,1,0:T(8,128)(2,1)S(1)}, u32[]{:S(2)}, u32[]{:S(2)}) %collective-permute-start.10) | collective-permute-done | bytes 540704 | tf_op jit(solution)/shard_map/ppermute | solution.py:427
  89.6 1.2 add_convert_fusion
  90.8 0.1 collective-permute-start.11
  90.9 2.7 %collective-permute-start.13 = (bf16[264,256]{1,0:T(8,128)(2,1)S(1)}, bf16[264,256]{1,0:T(8,128)(2,1)S(1)}, u32[]{:S(2)}, u32[]{:S(2)}) collective-permute-start(bf16[264,256]{1,0:T(8,128)(2,1)S(1)} %get-tuple-element.31), channel_id=1, source_target_pairs={{0,6},{1,7},{2,0},{3,1},{4,2},{5,3},{6,4},{7,5},{8,14},{9,15},{10,... | collective-permute-start | bytes 405512 | tf_op jit(solution)/shard_map/ppermute | solution.py:429
  93.6 0.5 collective-permute-start.12
  94.1 3.0 %collective-permute-done.11 = bf16[264,256]{1,0:T(8,128)(2,1)S(1)} collective-permute-done((bf16[264,256]{1,0:T(8,128)(2,1)S(1)}, bf16[264,256]{1,0:T(8,128)(2,1)S(1)}, u32[]{:S(2)}, u32[]{:S(2)}) %collective-permute-start.11) | collective-permute-done | bytes 135200 | tf_op jit(solution)/shard_map/ppermute | solution.py:429
  97.1 1.8 %collective-permute-done.13 = bf16[264,256]{1,0:T(8,128)(2,1)S(1)} collective-permute-done((bf16[264,256]{1,0:T(8,128)(2,1)S(1)}, bf16[264,256]{1,0:T(8,128)(2,1)S(1)}, u32[]{:S(2)}, u32[]{:S(2)}) %collective-permute-start.13) | collective-permute-done | bytes 135200 | tf_op jit(solution)/shard_map/ppermute | solution.py:429
  98.9 0.6 collective-permute-done.12
  99.5 0.1 fusion.2
  99.7 10.1 %all_to_all.15 = bf16[16,24,256]{2,1,0:T(8,128)(2,1)S(1)} all-to-all(bf16[16,24,256]{2,1,0:T(8,128)(2,1)S(1)} %pad_maximum_fusion), channel_id=1, replica_groups=mesh['grp'=2,'dp'=16,'row'=8] {'dp'}, dimensions={0} | all-to-all | bytes 393216 | tf_op jit(solution)/shard_map/all_to_all | solution.py:437
  109.9 12.3 %all_to_all.16.done = bf16[8,24,256]{2,1,0:T(8,128)(2,1)} all-to-all(bf16[8,24,256]{2,1,0:T(8,128)(2,1)S(1)} %broadcast_in_dim.5), channel_id=1, replica_groups=mesh['grp'=2,'dp'=16,'row'=8] {'row'}, dimensions={0} | all-to-all | bytes 196608 | tf_op jit(solution)/shard_map/all_to_all | solution.py:397
  122.1 1.6 %finish.1 = (f32[1,16,1024]{2,1,0:T(8,128)}, f32[1,64,256]{2,1,0:T(8,128)}, f32[7,7,1,256]{3,2,1,0:T(1,128)}, f32[1,256]{1,0:T(1,128)}, f32[1,256]{1,0:T(1,128)}) custom-call(bf16[8,24,256]{2,1,0:T(8,128)(2,1)} %all_to_all.16.done), custom_call_target="tpu_custom_call" | custom-call | tf_op jit(solution)/shard_map/finish/pallas_call | solution.py:85
  (20 shorter events, 0.1 us)
Async XLA Ops:
  3.5 24.0 %all-to-all-start = ((bf16[32,16,256]{2,1,0:T(8,128)(2,1)}), bf16[32,16,256]{2,1,0:T(8,128)(2,1)S(1)}, u32[]{:S(2)}, u32[]{:S(2)}) async-start(bf16[32,16,256]{2,1,0:T(8,128)(2,1)} %get-tuple-element.18), calls=%async_computation | async-start | bytes 524288 | tf_op jit(solution)/shard_map/all_to_all | solution.py:415
  15.6 27.0 %collective-permute-start.7 = (bf16[3,256,256]{2,1,0:T(8,128)(2,1)}, bf16[3,256,256]{2,1,0:T(8,128)(2,1)S(1)}, u32[]{:S(2)}, u32[]{:S(2)}) collective-permute-start(bf16[3,256,256]{2,1,0:T(8,128)(2,1)} %get-tuple-element.19), channel_id=1, source_target_pairs={{0,1},{1,2},{2,3},{3,4},{4,5},{5,6},{6,7},{7,0},{8,9},{9,10},{10,1... | collective-permute-start | bytes 1179656 | tf_op jit(solution)/shard_map/ppermute | solution.py:412
  27.5 36.2 %copy-start.2 = (bf16[32,16,256]{2,1,0:T(8,128)(2,1)}, bf16[32,16,256]{2,1,0:T(8,128)(2,1)S(1)}, u32[]{:S(2)}) copy-start(bf16[32,16,256]{2,1,0:T(8,128)(2,1)S(1)} %all-to-all-done.refs_0_) | copy-start | bytes 786436
  27.5 15.2 %collective-permute-start.5 = (bf16[32,16,256]{2,1,0:T(8,128)(2,1)S(1)}, bf16[32,16,256]{2,1,0:T(8,128)(2,1)S(1)}, u32[]{:S(2)}, u32[]{:S(2)}) collective-permute-start(bf16[32,16,256]{2,1,0:T(8,128)(2,1)S(1)} %all-to-all-done.refs_0_), channel_id=1, source_target_pairs={{0,6},{1,7},{2,0},{3,1},{4,2},{5,3},{6,4},{7,5},{8,14},{9,15},{10,... | collective-permute-start | bytes 786440 | tf_op jit(solution)/shard_map/ppermute | solution.py:416
  30.0 13.1 %collective-permute-start.3 = (bf16[32,16,256]{2,1,0:T(8,128)(2,1)S(1)}, bf16[32,16,256]{2,1,0:T(8,128)(2,1)S(1)}, u32[]{:S(2)}, u32[]{:S(2)}) collective-permute-start(bf16[32,16,256]{2,1,0:T(8,128)(2,1)S(1)} %all-to-all-done.refs_0_), channel_id=1, source_target_pairs={{0,4},{1,5},{2,6},{3,7},{4,0},{5,1},{6,2},{7,3},{8,12},{9,13},{10,... | collective-permute-start | bytes 786440 | tf_op jit(solution)/shard_map/ppermute | solution.py:416
  30.5 14.2 %collective-permute-start.1 = (bf16[32,16,256]{2,1,0:T(8,128)(2,1)S(1)}, bf16[32,16,256]{2,1,0:T(8,128)(2,1)S(1)}, u32[]{:S(2)}, u32[]{:S(2)}) collective-permute-start(bf16[32,16,256]{2,1,0:T(8,128)(2,1)S(1)} %all-to-all-done.refs_0_), channel_id=1, source_target_pairs={{0,2},{1,3},{2,4},{3,5},{4,6},{5,7},{6,0},{7,1},{8,10},{9,11},{10,... | collective-permute-start | bytes 786440 | tf_op jit(solution)/shard_map/ppermute | solution.py:416
  31.2 6.9 %collective-permute-start.9 = (bf16[64,256]{1,0:T(8,128)(2,1)}, bf16[64,256]{1,0:T(8,128)(2,1)S(1)}, u32[]{:S(2)}, u32[]{:S(2)}) collective-permute-start(bf16[64,256]{1,0:T(8,128)(2,1)} %get-tuple-element.21.own.refs_13_), channel_id=1, source_target_pairs={{0,128},{128,0},{1,129},{129,1},{2,130},{130,2},{3,131},{131,3},{4... | collective-permute-start | bytes 98312 | tf_op jit(solution)/shard_map/ppermute | solution.py:414
  38.0 11.7 %copy-start.3 = (bf16[64,256]{1,0:T(8,128)(2,1)}, bf16[64,256]{1,0:T(8,128)(2,1)S(1)}, u32[]{:S(2)}) copy-start(bf16[64,256]{1,0:T(8,128)(2,1)S(1)} %collective-permute-done.9.men.refs_14_) | copy-start | bytes 98308
  38.0 11.7 %collective-permute-start.8 = (bf16[3,256,256]{2,1,0:T(8,128)(2,1)}, bf16[3,256,256]{2,1,0:T(8,128)(2,1)S(1)}, u32[]{:S(2)}, u32[]{:S(2)}) collective-permute-start(bf16[3,256,256]{2,1,0:T(8,128)(2,1)} %get-tuple-element.20), channel_id=1, source_target_pairs={{0,7},{1,0},{2,1},{3,2},{4,3},{5,4},{6,5},{7,6},{8,15},{9,8},{10,9... | collective-permute-start | bytes 1179656 | tf_op jit(solution)/shard_map/ppermute | solution.py:413
  42.6 7.1 %copy-start = (bf16[3,256,256]{2,1,0:T(8,128)(2,1)}, bf16[3,256,256]{2,1,0:T(8,128)(2,1)S(1)}, u32[]{:S(2)}) copy-start(bf16[3,256,256]{2,1,0:T(8,128)(2,1)S(1)} %collective-permute-done.7.top.refs_11_) | copy-start | bytes 1179652
  42.6 21.1 %collective-permute-start = (bf16[32,16,256]{2,1,0:T(8,128)(2,1)S(1)}, bf16[32,16,256]{2,1,0:T(8,128)(2,1)S(1)}, u32[]{:S(2)}, u32[]{:S(2)}) collective-permute-start(bf16[32,16,256]{2,1,0:T(8,128)(2,1)S(1)} %all-to-all-done.refs_0_), channel_id=1, source_target_pairs={{0,1},{1,0},{2,3},{3,2},{4,5},{5,4},{6,7},{7,6},{8,9},{9,8},{10,11... | collective-permute-start | bytes 786440 | tf_op jit(solution)/shard_map/ppermute | solution.py:419
  42.7 21.0 %copy-start.4 = (bf16[32,16,256]{2,1,0:T(8,128)(2,1)}, bf16[32,16,256]{2,1,0:T(8,128)(2,1)S(1)}, u32[]{:S(2)}) copy-start(bf16[32,16,256]{2,1,0:T(8,128)(2,1)S(1)} %collective-permute-done.5.refs_6_) | copy-start | bytes 786436
  42.7 21.0 %collective-permute-start.6 = (bf16[32,16,256]{2,1,0:T(8,128)(2,1)S(1)}, bf16[32,16,256]{2,1,0:T(8,128)(2,1)S(1)}, u32[]{:S(2)}, u32[]{:S(2)}) collective-permute-start(bf16[32,16,256]{2,1,0:T(8,128)(2,1)S(1)} %collective-permute-done.5.refs_6_), channel_id=1, source_target_pairs={{0,1},{1,0},{2,3},{3,2},{4,5},{5,4},{6,7},{7,6},{8,9},{9,8},{10,11... | collective-permute-start | bytes 786440 | tf_op jit(solution)/shard_map/ppermute | solution.py:419
  43.1 20.6 %copy-start.5 = (bf16[32,16,256]{2,1,0:T(8,128)(2,1)}, bf16[32,16,256]{2,1,0:T(8,128)(2,1)S(1)}, u32[]{:S(2)}) copy-start(bf16[32,16,256]{2,1,0:T(8,128)(2,1)S(1)} %collective-permute-done.3.refs_4_) | copy-start | bytes 786436
  43.1 20.6 %collective-permute-start.4 = (bf16[32,16,256]{2,1,0:T(8,128)(2,1)S(1)}, bf16[32,16,256]{2,1,0:T(8,128)(2,1)S(1)}, u32[]{:S(2)}, u32[]{:S(2)}) collective-permute-start(bf16[32,16,256]{2,1,0:T(8,128)(2,1)S(1)} %collective-permute-done.3.refs_4_), channel_id=1, source_target_pairs={{0,1},{1,0},{2,3},{3,2},{4,5},{5,4},{6,7},{7,6},{8,9},{9,8},{10,11... | collective-permute-start | bytes 786440 | tf_op jit(solution)/shard_map/ppermute | solution.py:419
  44.7 19.0 %copy-start.6 = (bf16[32,16,256]{2,1,0:T(8,128)(2,1)}, bf16[32,16,256]{2,1,0:T(8,128)(2,1)S(1)}, u32[]{:S(2)}) copy-start(bf16[32,16,256]{2,1,0:T(8,128)(2,1)S(1)} %collective-permute-done.1.refs_2_) | copy-start | bytes 786436
  44.7 19.1 %collective-permute-start.2 = (bf16[32,16,256]{2,1,0:T(8,128)(2,1)S(1)}, bf16[32,16,256]{2,1,0:T(8,128)(2,1)S(1)}, u32[]{:S(2)}, u32[]{:S(2)}) collective-permute-start(bf16[32,16,256]{2,1,0:T(8,128)(2,1)S(1)} %collective-permute-done.1.refs_2_), channel_id=1, source_target_pairs={{0,1},{1,0},{2,3},{3,2},{4,5},{5,4},{6,7},{7,6},{8,9},{9,8},{10,11... | collective-permute-start | bytes 786440 | tf_op jit(solution)/shard_map/ppermute | solution.py:419
  49.7 0.8 copy-start.1
  63.7 0.7 copy-start.7
  63.8 0.8 copy-start.8
  63.8 0.9 copy-start.9
  64.7 0.7 copy-start.10
  87.4 2.2 %collective-permute-start.10 = (bf16[4,264,256]{2,1,0:T(8,128)(2,1)}, bf16[4,264,256]{2,1,0:T(8,128)(2,1)S(1)}, u32[]{:S(2)}, u32[]{:S(2)}) collective-permute-start(bf16[4,264,256]{2,1,0:T(8,128)(2,1)} %get-tuple-element.24), channel_id=1, source_target_pairs={{0,1},{1,0},{2,3},{3,2},{4,5},{5,4},{6,7},{7,6},{8,9},{9,8},{10,11... | collective-permute-start | bytes 1622024 | tf_op jit(solution)/shard_map/ppermute | solution.py:427
  90.8 6.3 %collective-permute-start.11 = (bf16[264,256]{1,0:T(8,128)(2,1)S(1)}, bf16[264,256]{1,0:T(8,128)(2,1)S(1)}, u32[]{:S(2)}, u32[]{:S(2)}) collective-permute-start(bf16[264,256]{1,0:T(8,128)(2,1)S(1)} %get-tuple-element.30), channel_id=1, source_target_pairs={{0,2},{1,3},{2,4},{3,5},{4,6},{5,7},{6,0},{7,1},{8,10},{9,11},{10,... | collective-permute-start | bytes 405512 | tf_op jit(solution)/shard_map/ppermute | solution.py:429
  90.9 8.0 %collective-permute-start.13 = (bf16[264,256]{1,0:T(8,128)(2,1)S(1)}, bf16[264,256]{1,0:T(8,128)(2,1)S(1)}, u32[]{:S(2)}, u32[]{:S(2)}) collective-permute-start(bf16[264,256]{1,0:T(8,128)(2,1)S(1)} %get-tuple-element.31), channel_id=1, source_target_pairs={{0,6},{1,7},{2,0},{3,1},{4,2},{5,3},{6,4},{7,5},{8,14},{9,15},{10,... | collective-permute-start | bytes 405512 | tf_op jit(solution)/shard_map/ppermute | solution.py:429
  93.6 6.0 %collective-permute-start.12 = (bf16[264,256]{1,0:T(8,128)(2,1)S(1)}, bf16[264,256]{1,0:T(8,128)(2,1)S(1)}, u32[]{:S(2)}, u32[]{:S(2)}) collective-permute-start(bf16[264,256]{1,0:T(8,128)(2,1)S(1)} %get-tuple-element.32), channel_id=1, source_target_pairs={{0,4},{1,5},{2,6},{3,7},{4,0},{5,1},{6,2},{7,3},{8,12},{9,13},{10,... | collective-permute-start | bytes 405512 | tf_op jit(solution)/shard_map/ppermute | solution.py:429
